TPU v7x, 32 devices: a whole 2x2x4 slice. The times are simulated.
32 devices in a mesh: row: 4 (over x, core), col: 8 (over z, y).
Axes of the slice: x: 2, y: 2, z: 4, core: 2. Of those that a mesh axis runs over, the one named last changes fastest.
Arguments:
- block_input: bfloat16 [8, 1024, 1024], P('col', 'row'), may hold values from -6 to 6
- state_start: bfloat16 [8, 512, 1024], P('col'), may hold values from -6 to 6
- teacher: bfloat16 [8, 1024, 1024], P('col', 'row'), may hold values from -6 to 6
- valid_mask: int32 [8, 1024], replicated, may hold values 0 or 1
- segment: int32 [8, 1024], P('col'), may hold values from 0 to 3, never falling along the last dimension, each value on 1 to 512 neighbouring positions
- image_offset: int32 [8, 2], P('col'), may hold values from 0 to 256
- retain: float32 [1024], replicated, may hold values from 0.55 to 0.995
- to_query: bfloat16 [1024, 1024], P('col', 'row'), may hold values from -0.1875 to 0.1875
- to_key: bfloat16 [1024, 1024], P('col', 'row'), may hold values from -0.1875 to 0.1875
- to_value: bfloat16 [1024, 1024], P('col', 'row'), may hold values from -0.1875 to 0.1875
- to_output: bfloat16 [1024, 1024], P('row', 'col'), may hold values from -4 to 4
- to_hidden: bfloat16 [1024, 4096], P('col'), may hold values from -0.1875 to 0.1875
- to_model: bfloat16 [4096, 1024], P(None, 'col'), may hold values from -0.09375 to 0.09375
- state_query: bfloat16 [1024, 1024], P('col', 'row'), may hold values from -0.1875 to 0.1875
- state_key: bfloat16 [1024, 1024], P('col', 'row'), may hold values from -0.1875 to 0.1875
- state_value: bfloat16 [1024, 1024], P('col', 'row'), may hold values from -0.1875 to 0.1875
- state_write: bfloat16 [1024, 1024], P(None, 'col'), may hold values from -4 to 4
- first_gain: float32 [1024], replicated, may hold values from 0.5 to 1.5
- second_gain: float32 [1024], replicated, may hold values from 0.5 to 1.5
- state_gain: float32 [1024], replicated, may hold values from 0.5 to 1.5
Outputs:
- total_loss: float32 [], replicated
- final_state: float32 [8, 512, 1024], P('col')
- input_grad: float32 [8, 1024, 1024], P('col', 'row')
- state_grad: float32 [8, 512, 1024], P('col')
- query_grad: float32 [1024, 1024], P('col', 'row')
- key_grad: float32 [1024, 1024], P('col', 'row')
- value_grad: float32 [1024, 1024], P('col', 'row')
- output_grad: float32 [1024, 1024], P('row', 'col')
- hidden_grad: float32 [1024, 4096], P('col', 'row')
- model_grad: float32 [4096, 1024], P('row', 'col')
- state_query_grad: float32 [1024, 1024], P('col', 'row')
- state_key_grad: float32 [1024, 1024], P('col', 'row')
- state_value_grad: float32 [1024, 1024], P('col', 'row')
- state_write_grad: float32 [1024, 1024], P('row', 'col')
- first_gain_grad: float32 [1024], replicated
- second_gain_grad: float32 [1024], replicated
- state_gain_grad: float32 [1024], replicated
Inputs may be any that keep to these rules, and one draw needn't show every extreme that they name: `image_offset`: each block's image piece starts at this offset from the block's first token and ends inside the block. `segment`: document numbers never fall along a sequence; every one of the 4 numbers appears in each sequence.
All inputs are finite; a program needn't handle non-finite values.
Results may differ from a plain program's by a relative error of at most 0.02.
Values may be sent and summed in bfloat16 or wider, within the bound.
No kernel may reach another device: no remote copies, remote signals or barrier semaphores. Data moves between devices by JAX's collectives and lax.ppermute only.
A program may use at most 192 MiB of HBM per device.

v0:
```python
import jax
import jax.numpy as jnp
from jax import lax
from jax.sharding import PartitionSpec as P

HEAD = 128
BLOCK = 512
NS = 512
PIECE = 256


epsilon = 1e-06
masked_value = -1e30


def norm_rows(values, scaling):
    inverse = lax.rsqrt(jnp.mean(values * values, axis=-1, keepdims=True) + epsilon)
    normed = values * inverse
    return (normed * scaling, normed, inverse)


def norm_back(upstream, normed, inverse, scaling):
    scaled = upstream * scaling
    inner = jnp.mean(scaled * normed, axis=-1, keepdims=True)
    return (inverse * (scaled - normed * inner), jnp.sum(upstream * normed, axis=0))


def matmul(former, latter):
    return jnp.dot(former, latter, preferred_element_type=jnp.float32)


def times_transposed(former, latter):
    return lax.dot_general(
        former, latter, (((1,), (1,)), ((), ())), preferred_element_type=jnp.float32
    )


def transposed_times(former, latter):
    return lax.dot_general(
        former, latter, (((0,), (0,)), ((), ())), preferred_element_type=jnp.float32
    )


def gelu_back(pre_gelu, upstream):
    unused, pull_back = jax.vjp(jax.nn.gelu, pre_gelu)
    return pull_back(upstream)[0]


def piece_number(offsets, length):
    numbers = jnp.arange(offsets.shape[0], dtype=jnp.int32)
    places = jnp.arange(length, dtype=jnp.int32)[:, None]
    starts = (numbers * BLOCK + offsets)[None, :]
    inside = (places >= starts) & (places < starts + PIECE)
    return jnp.sum(jnp.where(inside, numbers[None, :] + 1, 0), axis=1) - 1


def token_mask(number, valid_pad, segment_pad, piece_pad):
    first_row = number * BLOCK
    row_places = first_row + jnp.arange(BLOCK, dtype=jnp.int32)
    col_places = first_row - BLOCK + jnp.arange(2 * BLOCK, dtype=jnp.int32)
    row_segment = lax.dynamic_slice_in_dim(segment_pad, first_row + BLOCK, BLOCK)
    row_piece = lax.dynamic_slice_in_dim(piece_pad, first_row + BLOCK, BLOCK)
    col_segment = lax.dynamic_slice_in_dim(segment_pad, first_row, 2 * BLOCK)
    col_piece = lax.dynamic_slice_in_dim(piece_pad, first_row, 2 * BLOCK)
    col_valid = lax.dynamic_slice_in_dim(valid_pad, first_row, 2 * BLOCK)
    nearby = row_places[:, None] - col_places[None, :] < BLOCK
    earlier = col_places[None, :] <= row_places[:, None]
    same_piece = (row_piece[:, None] == col_piece[None, :]) & (row_piece[:, None] >= 0)
    allowed = (
        (col_valid[None, :] > 0)
        & (row_segment[:, None] == col_segment[None, :])
        & nearby
        & (earlier | same_piece)
    )
    return jnp.concatenate([allowed, jnp.full((BLOCK, NS), True)], axis=1)


def state_mask(number, valid_row):
    col_valid = lax.dynamic_slice_in_dim(valid_row, number * BLOCK, BLOCK) > 0
    joined = jnp.concatenate([col_valid, jnp.full((NS,), True)])
    return jnp.broadcast_to(joined[None, :], (NS, BLOCK + NS))


def scores_of(query_rows, key_rows, allowed, score_scale):
    logits = (
        jnp.einsum("rhe,khe->hrk", query_rows, key_rows, preferred_element_type=jnp.float32)
        * score_scale
    )
    return jnp.where(allowed[None], logits, masked_value)


def attend(query_rows, key_rows, value_rows, allowed, score_scale):
    logits = scores_of(query_rows, key_rows, allowed, score_scale)
    largest = jnp.max(logits, axis=-1, keepdims=True)
    raised = jnp.exp(logits - largest)
    totals = jnp.sum(raised, axis=-1, keepdims=True)
    chances = raised / totals
    mixture = jnp.einsum(
        "hrk,khe->rhe", chances.astype(jnp.bfloat16), value_rows, preferred_element_type=jnp.float32
    )
    return (mixture.astype(jnp.bfloat16), largest[..., 0] + jnp.log(totals[..., 0]))


def attend_back(query_rows, key_rows, value_rows, allowed, score_scale, log_total, grad_mixture):
    logits = scores_of(query_rows, key_rows, allowed, score_scale)
    chances = jnp.exp(logits - log_total[..., None])
    grad_chance = jnp.einsum(
        "rhe,khe->hrk", grad_mixture, value_rows, preferred_element_type=jnp.float32
    )
    inner = jnp.sum(chances * grad_chance, axis=-1, keepdims=True)
    grad_logit = (chances * (grad_chance - inner)).astype(jnp.bfloat16)
    grad_query = (
        jnp.einsum("hrk,khe->rhe", grad_logit, key_rows, preferred_element_type=jnp.float32)
        * score_scale
    )
    grad_key = (
        jnp.einsum("hrk,rhe->khe", grad_logit, query_rows, preferred_element_type=jnp.float32)
        * score_scale
    )
    grad_value = jnp.einsum(
        "hrk,rhe->khe",
        chances.astype(jnp.bfloat16),
        grad_mixture,
        preferred_element_type=jnp.float32,
    )
    return (grad_query, grad_key, grad_value)


def per_device(
    block_input,
    state_start,
    teacher,
    valid_mask,
    segment,
    image_offset,
    retain,
    to_query,
    to_key,
    to_value,
    to_output,
    to_hidden,
    to_model,
    state_query,
    state_key,
    state_value,
    state_write,
    first_gain,
    second_gain,
    state_gain,
):
    row_devices = lax.axis_size("row")
    col_devices = lax.axis_size("col")
    row_index = lax.axis_index("row")
    col_index = lax.axis_index("col")
    tokens = block_input[0].astype(jnp.float32)
    local_rows = tokens.shape[0]
    length = local_rows * row_devices
    local_width = to_query.shape[1]
    heads_here = local_width // HEAD
    hidden_here = to_hidden.shape[1] // row_devices
    score_scale = HEAD ** (-0.5)
    nblocks = length // BLOCK
    blocks = jnp.arange(nblocks, dtype=jnp.int32)
    upper_part = lax.dynamic_slice_in_dim(to_hidden, row_index * hidden_here, hidden_here, 1)
    lower_part = lax.dynamic_slice_in_dim(to_model, row_index * hidden_here, hidden_here, 0)
    gathered = (
        lax.all_gather(to_query, "col", axis=0, tiled=True),
        lax.all_gather(to_key, "col", axis=0, tiled=True),
        lax.all_gather(to_value, "col", axis=0, tiled=True),
        lax.all_gather(to_output, "col", axis=1, tiled=True),
        lax.all_gather(upper_part, "col", axis=0, tiled=True),
        lax.all_gather(lower_part, "col", axis=1, tiled=True),
        lax.all_gather(state_query, "col", axis=0, tiled=True),
        lax.all_gather(state_key, "col", axis=0, tiled=True),
        lax.all_gather(state_value, "col", axis=0, tiled=True),
        lax.all_gather(state_write, "col", axis=1, tiled=True),
    )
    token_proj = jnp.concatenate([gathered[0], gathered[1], gathered[2]], axis=1)
    output_proj = gathered[3]
    upper_proj = gathered[4]
    lower_proj = gathered[5]
    state_proj = jnp.concatenate([gathered[6], gathered[7], gathered[8]], axis=1)
    write_proj = gathered[9]
    write_mine = lax.dynamic_slice_in_dim(write_proj, row_index * local_width, local_width, 0)
    valid_row = lax.dynamic_index_in_dim(valid_mask, col_index, 0, keepdims=False)
    segment_row = segment[0]
    pieces = piece_number(image_offset[0], length)
    valid_pad = jnp.pad(valid_row, (BLOCK, 0))
    segment_pad = jnp.pad(segment_row, (BLOCK, 0), constant_values=-1)
    piece_pad = jnp.pad(pieces, (BLOCK, 0), constant_values=-1)
    local_valid = lax.dynamic_slice_in_dim(valid_row, row_index * local_rows, local_rows).astype(
        jnp.float32
    )
    valid_count = jnp.sum(valid_mask.astype(jnp.float32))
    first_normed, first_unit, first_inverse = norm_rows(tokens, first_gain)
    first_all = lax.all_gather(first_normed.astype(jnp.bfloat16), "row", axis=0, tiled=True)
    token_heads = matmul(first_all, token_proj).astype(jnp.bfloat16)
    query_all = token_heads[:, :local_width].reshape(length, heads_here, HEAD)
    key_all = token_heads[:, local_width : 2 * local_width].reshape(length, heads_here, HEAD)
    value_all = token_heads[:, 2 * local_width :].reshape(length, heads_here, HEAD)

    def state_split(state_trio):
        return (
            state_trio[:, :local_width].reshape(NS, heads_here, HEAD),
            state_trio[:, local_width : 2 * local_width].reshape(NS, heads_here, HEAD),
            state_trio[:, 2 * local_width :].reshape(NS, heads_here, HEAD),
        )

    def state_inputs(number, state_trio):
        state_queries, state_keys, state_values = state_split(state_trio)
        first_row = number * BLOCK
        key_rows = jnp.concatenate(
            [lax.dynamic_slice_in_dim(key_all, first_row, BLOCK), state_keys]
        )
        value_rows = jnp.concatenate(
            [lax.dynamic_slice_in_dim(value_all, first_row, BLOCK), state_values]
        )
        return (state_queries, key_rows, value_rows)

    def chain_step(current, number):
        state_normed = norm_rows(current, state_gain)[0].astype(jnp.bfloat16)
        state_trio = matmul(state_normed, state_proj).astype(jnp.bfloat16)
        state_queries, key_rows, value_rows = state_inputs(number, state_trio)
        mixture, log_total = attend(
            state_queries, key_rows, value_rows, state_mask(number, valid_row), score_scale
        )
        heads_out = mixture.reshape(NS, local_width)
        all_heads = lax.all_gather(heads_out, "row", axis=1, tiled=True)
        update = matmul(all_heads, write_proj)
        following = retain * current + (1.0 - retain) * update
        return (following, (current, state_trio, heads_out, log_total))

    final_state, (state_stack, trio_stack, heads_stack, state_logs) = lax.scan(
        chain_step, state_start[0].astype(jnp.float32), blocks
    )
    key_pad = jnp.pad(key_all, ((BLOCK, 0), (0, 0), (0, 0)))
    value_pad = jnp.pad(value_all, ((BLOCK, 0), (0, 0), (0, 0)))

    def token_inputs(number, state_trio):
        unused, state_keys, state_values = state_split(state_trio)
        first_row = number * BLOCK
        query_rows = lax.dynamic_slice_in_dim(query_all, first_row, BLOCK)
        key_rows = jnp.concatenate(
            [lax.dynamic_slice_in_dim(key_pad, first_row, 2 * BLOCK), state_keys]
        )
        value_rows = jnp.concatenate(
            [lax.dynamic_slice_in_dim(value_pad, first_row, 2 * BLOCK), state_values]
        )
        return (query_rows, key_rows, value_rows)

    def token_step(carried, element):
        number, state_trio = element
        query_rows, key_rows, value_rows = token_inputs(number, state_trio)
        mixture, log_total = attend(
            query_rows,
            key_rows,
            value_rows,
            token_mask(number, valid_pad, segment_pad, piece_pad),
            score_scale,
        )
        return (carried, (mixture, log_total))

    unused, (token_mixture, token_logs) = lax.scan(
        token_step, jnp.zeros((), jnp.int32), (blocks, trio_stack)
    )
    mixture_all = token_mixture.reshape(length, local_width)
    attend_sum = lax.psum_scatter(
        matmul(mixture_all, output_proj).astype(jnp.bfloat16),
        "row",
        scatter_dimension=0,
        tiled=True,
    ).astype(jnp.float32)
    after_attend = tokens + attend_sum
    second_normed, second_unit, second_inverse = norm_rows(after_attend, second_gain)
    second_low = second_normed.astype(jnp.bfloat16)
    dense_inputs = lax.all_gather(second_low, "row", axis=0, tiled=True)
    pre_gelu = matmul(dense_inputs, upper_proj)
    hidden_low = jax.nn.gelu(pre_gelu).astype(jnp.bfloat16)
    dense_sum = lax.psum_scatter(
        matmul(hidden_low, lower_proj).astype(jnp.bfloat16), "row", scatter_dimension=0, tiled=True
    ).astype(jnp.float32)
    block_out = after_attend + dense_sum
    errors = block_out - teacher[0].astype(jnp.float32)
    squared = jnp.sum(local_valid[:, None] * errors * errors)
    total_tokens = jnp.float32(length * col_devices)
    grad_output = total_tokens / valid_count * local_valid[:, None] * errors
    grad_dense = grad_output.astype(jnp.bfloat16)
    grad_gathered = lax.all_gather(grad_dense, "row", axis=0, tiled=True)
    grad_hidden = times_transposed(grad_gathered, lower_proj)
    lower_grad = transposed_times(hidden_low, grad_gathered)
    grad_pre = gelu_back(pre_gelu, grad_hidden).astype(jnp.bfloat16)
    upper_grad = transposed_times(dense_inputs, grad_pre)
    grad_second = lax.psum_scatter(
        times_transposed(grad_pre, upper_proj).astype(jnp.bfloat16),
        "row",
        scatter_dimension=0,
        tiled=True,
    ).astype(jnp.float32)
    grad_norm, second_grad = norm_back(grad_second, second_unit, second_inverse, second_gain)
    grad_after = grad_output + grad_norm
    grad_rows = lax.all_gather(grad_after.astype(jnp.bfloat16), "row", axis=0, tiled=True)
    output_grad = transposed_times(mixture_all, grad_rows)
    grad_mixture = (
        times_transposed(grad_rows, output_proj)
        .astype(jnp.bfloat16)
        .reshape(length, heads_here, HEAD)
    )

    def token_back(carried, element):
        key_sums, value_sums = carried
        number, state_trio, log_total = element
        query_rows, key_rows, value_rows = token_inputs(number, state_trio)
        first_row = number * BLOCK
        upstream = lax.dynamic_slice_in_dim(grad_mixture, first_row, BLOCK)
        grad_query, grad_key, grad_value = attend_back(
            query_rows,
            key_rows,
            value_rows,
            token_mask(number, valid_pad, segment_pad, piece_pad),
            score_scale,
            log_total,
            upstream,
        )
        key_sums = lax.dynamic_update_slice_in_dim(
            key_sums,
            lax.dynamic_slice_in_dim(key_sums, first_row, 2 * BLOCK) + grad_key[: 2 * BLOCK],
            first_row,
            0,
        )
        value_sums = lax.dynamic_update_slice_in_dim(
            value_sums,
            lax.dynamic_slice_in_dim(value_sums, first_row, 2 * BLOCK) + grad_value[: 2 * BLOCK],
            first_row,
            0,
        )
        return (
            (key_sums, value_sums),
            (grad_query, grad_key[2 * BLOCK :], grad_value[2 * BLOCK :]),
        )

    zero_rows = jnp.zeros((length + BLOCK, heads_here, HEAD), jnp.float32)
    (key_sums, value_sums), (query_grads, key_extra, value_extra) = lax.scan(
        token_back, (zero_rows, zero_rows), (blocks, trio_stack, token_logs)
    )

    def chain_back(carried, element):
        grad_next, key_sums, value_sums, write_grad, trio_grad, gain_sums = carried
        number, current, state_trio, heads_out, log_total, extra_keys, extra_values = element
        grad_update = ((1.0 - retain) * grad_next).astype(jnp.bfloat16)
        write_grad = write_grad + transposed_times(heads_out, grad_update)
        grad_heads = (
            times_transposed(grad_update, write_mine)
            .astype(jnp.bfloat16)
            .reshape(NS, heads_here, HEAD)
        )
        state_queries, key_rows, value_rows = state_inputs(number, state_trio)
        grad_query, grad_key, grad_value = attend_back(
            state_queries,
            key_rows,
            value_rows,
            state_mask(number, valid_row),
            score_scale,
            log_total,
            grad_heads,
        )
        first_row = number * BLOCK + BLOCK
        key_sums = lax.dynamic_update_slice_in_dim(
            key_sums,
            lax.dynamic_slice_in_dim(key_sums, first_row, BLOCK) + grad_key[:BLOCK],
            first_row,
            0,
        )
        value_sums = lax.dynamic_update_slice_in_dim(
            value_sums,
            lax.dynamic_slice_in_dim(value_sums, first_row, BLOCK) + grad_value[:BLOCK],
            first_row,
            0,
        )
        grad_trio = jnp.concatenate(
            [
                grad_query.reshape(NS, local_width),
                (grad_key[BLOCK:] + extra_keys).reshape(NS, local_width),
                (grad_value[BLOCK:] + extra_values).reshape(NS, local_width),
            ],
            axis=1,
        ).astype(jnp.bfloat16)
        state_normed, state_unit, state_inverse = norm_rows(current, state_gain)
        trio_grad = trio_grad + transposed_times(state_normed.astype(jnp.bfloat16), grad_trio)
        grad_normed = times_transposed(grad_trio, state_proj)
        gain_sums = gain_sums + jnp.sum(grad_normed * state_unit, axis=0)
        grad_normed = lax.psum(grad_normed.astype(jnp.bfloat16), "row").astype(jnp.float32)
        grad_state, unused = norm_back(grad_normed, state_unit, state_inverse, state_gain)
        return (
            (
                retain * grad_next + grad_state,
                key_sums,
                value_sums,
                write_grad,
                trio_grad,
                gain_sums,
            ),
            None,
        )

    width = tokens.shape[1]
    start_carry = (
        jnp.zeros((NS, width), jnp.float32),
        key_sums,
        value_sums,
        jnp.zeros((local_width, width), jnp.float32),
        jnp.zeros((width, 3 * local_width), jnp.float32),
        jnp.zeros((width,), jnp.float32),
    )
    (grad_start, key_sums, value_sums, write_grad, trio_grad, gain_sums), unused = lax.scan(
        chain_back,
        start_carry,
        (blocks, state_stack, trio_stack, heads_stack, state_logs, key_extra, value_extra),
        reverse=True,
    )
    grad_heads_all = jnp.concatenate(
        [
            query_grads.reshape(length, local_width),
            key_sums[BLOCK:].reshape(length, local_width),
            value_sums[BLOCK:].reshape(length, local_width),
        ],
        axis=1,
    ).astype(jnp.bfloat16)
    token_grad = transposed_times(first_all, grad_heads_all)
    grad_first = lax.psum_scatter(
        times_transposed(grad_heads_all, token_proj).astype(jnp.bfloat16),
        "row",
        scatter_dimension=0,
        tiled=True,
    ).astype(jnp.float32)
    grad_norm_first, first_grad = norm_back(grad_first, first_unit, first_inverse, first_gain)
    input_grad = grad_after + grad_norm_first
    reduced = (
        lax.psum_scatter(
            token_grad[:, :local_width].astype(jnp.bfloat16), "col", scatter_dimension=0, tiled=True
        ).astype(jnp.float32),
        lax.psum_scatter(
            token_grad[:, local_width : 2 * local_width].astype(jnp.bfloat16),
            "col",
            scatter_dimension=0,
            tiled=True,
        ).astype(jnp.float32),
        lax.psum_scatter(
            token_grad[:, 2 * local_width :].astype(jnp.bfloat16),
            "col",
            scatter_dimension=0,
            tiled=True,
        ).astype(jnp.float32),
        lax.psum_scatter(
            output_grad.astype(jnp.bfloat16), "col", scatter_dimension=1, tiled=True
        ).astype(jnp.float32),
        lax.psum_scatter(
            upper_grad.astype(jnp.bfloat16), "col", scatter_dimension=0, tiled=True
        ).astype(jnp.float32),
        lax.psum_scatter(
            lower_grad.astype(jnp.bfloat16), "col", scatter_dimension=1, tiled=True
        ).astype(jnp.float32),
        lax.psum_scatter(
            trio_grad[:, :local_width].astype(jnp.bfloat16), "col", scatter_dimension=0, tiled=True
        ).astype(jnp.float32),
        lax.psum_scatter(
            trio_grad[:, local_width : 2 * local_width].astype(jnp.bfloat16),
            "col",
            scatter_dimension=0,
            tiled=True,
        ).astype(jnp.float32),
        lax.psum_scatter(
            trio_grad[:, 2 * local_width :].astype(jnp.bfloat16),
            "col",
            scatter_dimension=0,
            tiled=True,
        ).astype(jnp.float32),
        lax.psum_scatter(
            write_grad.astype(jnp.bfloat16), "col", scatter_dimension=1, tiled=True
        ).astype(jnp.float32),
    )
    upper_local = reduced[4]
    lower_local = reduced[5]
    summed = lax.psum((squared, first_grad, second_grad, gain_sums), ("row", "col"))
    total_loss = summed[0] / (2.0 * valid_count)
    return (
        total_loss,
        final_state[None],
        input_grad[None],
        grad_start[None],
        reduced[0],
        reduced[1],
        reduced[2],
        reduced[3],
        upper_local,
        lower_local,
        reduced[6],
        reduced[7],
        reduced[8],
        reduced[9],
        summed[1],
        summed[2],
        summed[3],
    )


def solution(mesh):
    in_specs = (
        P("col", "row", None),
        P("col", None, None),
        P("col", "row", None),
        P(),
        P("col", None),
        P("col", None),
        P(),
        P("col", "row"),
        P("col", "row"),
        P("col", "row"),
        P("row", "col"),
        P("col", None),
        P(None, "col"),
        P("col", "row"),
        P("col", "row"),
        P("col", "row"),
        P(None, "col"),
        P(),
        P(),
        P(),
    )
    out_specs = (
        P(),
        P("col", None, None),
        P("col", "row", None),
        P("col", None, None),
        P("col", "row"),
        P("col", "row"),
        P("col", "row"),
        P("row", "col"),
        P("col", "row"),
        P("row", "col"),
        P("col", "row"),
        P("col", "row"),
        P("col", "row"),
        P("row", "col"),
        P(),
        P(),
        P(),
    )
    return jax.shard_map(
        per_device, mesh=mesh, in_specs=in_specs, out_specs=out_specs, check_vma=False
    )
```

profile of v0, /device:TPU:0, one launch (start us, length us, event | category | flops | bytes accessed | tf_op | source)
XLA Modules:
  0.0 1585.9 jit_solution(11760355644158231017)
XLA Ops:
  13.0 33.1 %all_gather.46 = bf16[1024,256]{1,0:T(8,128)(2,1)S(1)} all-gather(bf16[128,256]{1,0:T(8,128)(2,1)S(1)} %copy-done.77), channel_id=1, replica_groups=mesh['row'=4,'col'=8] {'col'}, dimensions={0}, use_global_device_ids=true | all-gather | bytes 589824 | tf_op jit(solution)/shard_map/all_gather | solution.py:167
  46.2 32.6 %all_gather.49 = bf16[1024,256]{1,0:T(8,128)(2,1)S(1)} all-gather(bf16[128,256]{1,0:T(8,128)(2,1)S(1)} %copy-done.78), channel_id=1, replica_groups=mesh['row'=4,'col'=8] {'col'}, dimensions={0}, use_global_device_ids=true | all-gather | bytes 589824 | tf_op jit(solution)/shard_map/all_gather | solution.py:173
  79.6 32.3 %all_gather.47 = bf16[1024,256]{1,0:T(8,128)(2,1)S(1)} all-gather(bf16[128,256]{1,0:T(8,128)(2,1)S(1)} %copy-done.79), channel_id=1, replica_groups=mesh['row'=4,'col'=8] {'col'}, dimensions={0}, use_global_device_ids=true | all-gather | bytes 589824 | tf_op jit(solution)/shard_map/all_gather | solution.py:168
  112.0 31.5 %all_gather.48 = bf16[1024,256]{1,0:T(8,128)(2,1)S(1)} all-gather(bf16[128,256]{1,0:T(8,128)(2,1)S(1)} %copy-done.80), channel_id=1, replica_groups=mesh['row'=4,'col'=8] {'col'}, dimensions={0}, use_global_device_ids=true | all-gather | bytes 589824 | tf_op jit(solution)/shard_map/all_gather | solution.py:169
  143.6 31.7 %all_gather.50 = bf16[1024,256]{1,0:T(8,128)(2,1)S(1)} all-gather(bf16[128,256]{1,0:T(8,128)(2,1)S(1)} %copy-done.81), channel_id=1, replica_groups=mesh['row'=4,'col'=8] {'col'}, dimensions={0}, use_global_device_ids=true | all-gather | bytes 589824 | tf_op jit(solution)/shard_map/all_gather | solution.py:174
  176.1 31.4 %all_gather.51 = bf16[1024,256]{1,0:T(8,128)(2,1)S(1)} all-gather(bf16[128,256]{1,0:T(8,128)(2,1)S(1)} %copy-done.82), channel_id=1, replica_groups=mesh['row'=4,'col'=8] {'col'}, dimensions={0}, use_global_device_ids=true | all-gather | bytes 589824 | tf_op jit(solution)/shard_map/all_gather | solution.py:175
  208.7 28.1 %all_gather.53 = bf16[256,1024]{1,0:T(8,128)(2,1)} all-gather(bf16[256,128]{1,0:T(8,128)(2,1)S(1)} %copy-done.83), channel_id=1, replica_groups=mesh['row'=4,'col'=8] {'col'}, dimensions={1}, use_global_device_ids=true | all-gather | bytes 589824 | tf_op jit(solution)/shard_map/all_gather | solution.py:170
  249.1 65.1 %while.77 = (s32[]{:T(128)}, f32[512,1024]{1,0:T(8,128)}, f32[2,512,1024]{2,1,0:T(8,128)}, bf16[2,512,768]{1,2,0:T(8,128)(2,1)}, bf16[2,512,256]{1,2,0:T(8,128)(...) while((s32[]{:T(128)}, f32[512,1024]{1,0:T(8,128)}, ...), condition=%wide.region_5.6_spmd, body=%wide.region_1.0_spmd.sunk | while | flops 2435318784 | bytes 70847944 | solution.py:233
  264.1 12.0 all-gather.23.cloned.1.call-done
  296.1 12.9 all-gather.23.cloned.1.call-done
  315.6 36.8 %while.78 = (s32[]{:T(128)}, bf16[2,512,2,128]{3,2,1,0:T(2,128)(2,1)}, f32[2,2,512]{2,1,0:T(2,128)}, s32[2]{0:T(128)}, bf16[1536,2,128]{2,0,1:T(8,128)(2,1)}, /*...) while((s32[]{:T(128)}, ...), condition=%wide.region_10.11_spmd, body=%wide.region_7.10_spmd.sunk | while | flops 832702464 | bytes 67362992 | solution.py:263
  328.1 4.9 fusion.243
  346.5 4.9 fusion.243
  356.7 30.7 %reduce-scatter.21.cloned.1.call-done = bf16[256,1024]{1,0:T(8,128)(2,1)} async-done(((bf16[1024,1024]{1,0:T(8,128)(2,1)}), bf16[256,1024]{1,0:T(8,128)(2,1)}) %reduce-scatter.21.cloned.1.call-update) | async-done | bytes 524304 | tf_op jit(solution)/shard_map/reduce_scatter | solution.py:267
  392.5 46.9 %all-gather.15.cloned.1.call-done = bf16[1024,1024]{1,0:T(8,128)(2,1)} async-done(((bf16[128,1024]{1,0:T(8,128)(2,1)}), bf16[1024,1024]{1,0:T(8,128)(2,1)}) %all-gather.15.cloned.1.call-update) | async-done | bytes 2097168 | tf_op jit(solution)/shard_map/all_gather | solution.py:171
  439.4 23.3 %all-gather.13.cloned.1.call-done = bf16[1024,1024]{1,0:T(8,128)(2,1)} async-done(((bf16[256,1024]{1,0:T(8,128)(2,1)}), bf16[1024,1024]{1,0:T(8,128)(2,1)}) %all-gather.13.cloned.1.call-update) | async-done | bytes 2097168 | tf_op jit(solution)/shard_map/all_gather | solution.py:276
  462.7 6.6 fusion.151
  469.3 47.3 %all-gather.17.cloned.1.call-done = bf16[1024,1024]{1,0:T(8,128)(2,1)} async-done(((bf16[1024,128]{1,0:T(8,128)(2,1)}), bf16[1024,1024]{1,0:T(8,128)(2,1)}) %all-gather.17.cloned.1.call-update) | async-done | bytes 2097168 | tf_op jit(solution)/shard_map/all_gather | solution.py:172
  516.7 6.8 convolution_convert_fusion.5
  525.7 27.6 %reduce-scatter.23.cloned.1.call-done = bf16[256,1024]{1,0:T(8,128)(2,1)} async-done(((bf16[1024,1024]{1,0:T(8,128)(2,1)}), bf16[256,1024]{1,0:T(8,128)(2,1)}) %reduce-scatter.23.cloned.1.call-update) | async-done | bytes 524304 | tf_op jit(solution)/shard_map/reduce_scatter | solution.py:279
  555.5 22.7 %all-gather.19.cloned.1.call-done = bf16[1024,1024]{1,0:T(8,128)(2,1)} async-done(((bf16[256,1024]{1,0:T(8,128)(2,1)}), bf16[1024,1024]{1,0:T(8,128)(2,1)}) %all-gather.19.cloned.1.call-update) | async-done | bytes 2097168 | tf_op jit(solution)/shard_map/all_gather | solution.py:288
  578.2 8.1 fusion.112
  591.4 31.5 %reduce-scatter.25.cloned.1.call-done = bf16[256,1024]{1,0:T(8,128)(2,1)} async-done(((bf16[1024,1024]{1,0:T(8,128)(2,1)}), bf16[256,1024]{1,0:T(8,128)(2,1)}) %reduce-scatter.25.cloned.1.call-update) | async-done | bytes 524304 | tf_op jit(solution)/shard_map/reduce_scatter | solution.py:293
  629.2 5.6 convolution_convert_fusion.2
  637.5 12.5 all-gather.21.cloned.1.call-done
  655.1 57.4 %while.79 = (s32[]{:T(128)}, f32[1536,2,128]{0,2,1:T(8,128)}, f32[1536,2,128]{0,2,1:T(8,128)}, bf16[2,512,2,128]{1,3,2,0:T(8,128)(2,1)}, f32[2,512,2,128]{1,3,2,...) while((s32[]{:T(128)}, f32[1536,2,128]{0,2,1:T(8,128)}, ...), condition=%wide.region_21.22_spmd, body=%wide.region_19.21_spmd.sunk | while | flops 2038433792 | bytes 140324784 | solution.py:342
  669.8 4.7 multiply_reduce_fusion.12
  698.5 4.7 multiply_reduce_fusion.12
  712.5 128.4 %while.80 = (s32[]{:T(128)}, f32[512,1024]{1,0:T(8,128)}, f32[1536,2,128]{0,2,1:T(8,128)}, f32[1536,2,128]{0,2,1:T(8,128)}, f32[256,1024]{1,0:T(8,128)}, /*index...) while((s32[]{:T(128)}, f32[512,1024]{1,0:T(8,128)}, ...), condition=%wide.region_28.29_spmd.clone, body=%wide.region_22.28_spmd.clone.sunk | while | flops 3531999232 | bytes 168224336 | solution.py:414
  729.9 4.2 fusion.275
  741.7 28.7 %all-reduce.12.cloned.1.call-done = bf16[512,1024]{1,0:T(8,128)(2,1)} async-done(((bf16[512,1024]{1,0:T(8,128)(2,1)}), bf16[512,1024]{1,0:T(8,128)(2,1)}) %all-reduce.12.cloned.1.call-update) | async-done | bytes 1048592 | tf_op jit(solution)/shard_map/while/body/eval_jaxpr/psum | solution.py:391
  793.8 4.2 fusion.275
  802.6 5.0 select_add_fusion.4
  807.6 27.0 %all-reduce.12.cloned.1.call-done = bf16[512,1024]{1,0:T(8,128)(2,1)} async-done(((bf16[512,1024]{1,0:T(8,128)(2,1)}), bf16[512,1024]{1,0:T(8,128)(2,1)}) %all-reduce.12.cloned.1.call-update) | async-done | bytes 1048592 | tf_op jit(solution)/shard_map/while/body/eval_jaxpr/psum | solution.py:391
  842.5 5.3 convolution_convert_fusion.3
  869.7 4.5 convolution_convert_fusion.7
  875.0 38.7 %reduce-scatter.45.cloned.1.call-done = bf16[128,1024]{1,0:T(8,128)(2,1)} async-done(((bf16[1024,1024]{1,0:T(8,128)(2,1)}), bf16[128,1024]{1,0:T(8,128)(2,1)}) %reduce-scatter.45.cloned.1.call-update) | async-done | bytes 262160
  915.8 68.7 %reduce-scatter.35.cloned.1.call-done = bf16[128,1024]{1,0:T(8,128)(2,1)} async-done(((bf16[1024,1024]{1,0:T(8,128)(2,1)}), bf16[128,1024]{1,0:T(8,128)(2,1)}) %reduce-scatter.35.cloned.1.call-update) | async-done | bytes 262160 | tf_op jit(solution)/shard_map/reduce_scatter | solution.py:456
  986.3 62.7 %reduce-scatter.43.cloned.1.call-done = bf16[128,256]{1,0:T(8,128)(2,1)} async-done(((bf16[1024,256]{1,0:T(8,128)(2,1)}), bf16[128,256]{1,0:T(8,128)(2,1)}) %reduce-scatter.43.cloned.1.call-update) | async-done | bytes 65552
  1050.6 62.6 %reduce-scatter.47.cloned.1.call-done = bf16[128,256]{1,0:T(8,128)(2,1)} async-done(((bf16[1024,256]{1,0:T(8,128)(2,1)}), bf16[128,256]{1,0:T(8,128)(2,1)}) %reduce-scatter.47.cloned.1.call-update) | async-done | bytes 65552
  1114.8 63.0 %reduce-scatter.29.cloned.1.call-done = bf16[128,256]{1,0:T(8,128)(2,1)} async-done(((bf16[1024,256]{1,0:T(8,128)(2,1)}), bf16[128,256]{1,0:T(8,128)(2,1)}) %reduce-scatter.29.cloned.1.call-update) | async-done | bytes 65552 | tf_op jit(solution)/shard_map/reduce_scatter | solution.py:438
  1179.3 62.7 %reduce-scatter.31.cloned.1.call-done = bf16[128,256]{1,0:T(8,128)(2,1)} async-done(((bf16[1024,256]{1,0:T(8,128)(2,1)}), bf16[128,256]{1,0:T(8,128)(2,1)}) %reduce-scatter.31.cloned.1.call-update) | async-done | bytes 65552 | tf_op jit(solution)/shard_map/reduce_scatter | solution.py:441
  1243.5 63.7 %reduce-scatter.33.cloned.1.call-done = bf16[128,256]{1,0:T(8,128)(2,1)} async-done(((bf16[1024,256]{1,0:T(8,128)(2,1)}), bf16[128,256]{1,0:T(8,128)(2,1)}) %reduce-scatter.33.cloned.1.call-update) | async-done | bytes 65552 | tf_op jit(solution)/shard_map/reduce_scatter | solution.py:447
  1308.8 62.8 %reduce-scatter.37.cloned.1.call-done = bf16[128,256]{1,0:T(8,128)(2,1)} async-done(((bf16[1024,256]{1,0:T(8,128)(2,1)}), bf16[128,256]{1,0:T(8,128)(2,1)}) %reduce-scatter.37.cloned.1.call-update) | async-done | bytes 65552 | tf_op jit(solution)/shard_map/reduce_scatter | solution.py:462
  1373.1 63.2 %reduce-scatter.39.cloned.1.call-done = bf16[128,256]{1,0:T(8,128)(2,1)} async-done(((bf16[1024,256]{1,0:T(8,128)(2,1)}), bf16[128,256]{1,0:T(8,128)(2,1)}) %reduce-scatter.39.cloned.1.call-update) | async-done | bytes 65552 | tf_op jit(solution)/shard_map/reduce_scatter | solution.py:465
  1437.7 62.6 %reduce-scatter.41.cloned.1.call-done = bf16[128,256]{1,0:T(8,128)(2,1)} async-done(((bf16[1024,256]{1,0:T(8,128)(2,1)}), bf16[128,256]{1,0:T(8,128)(2,1)}) %reduce-scatter.41.cloned.1.call-update) | async-done | bytes 65552 | tf_op jit(solution)/shard_map/reduce_scatter | solution.py:471
  1502.0 31.6 %reduce-scatter.27.cloned.1.call-done = bf16[256,1024]{1,0:T(8,128)(2,1)} async-done(((bf16[1024,1024]{1,0:T(8,128)(2,1)}), bf16[256,1024]{1,0:T(8,128)(2,1)}) %reduce-scatter.27.cloned.1.call-update) | async-done | bytes 524304 | tf_op jit(solution)/shard_map/reduce_scatter | solution.py:429
  1535.1 39.7 %all-reduce.9 = (f32[]{:T(128)}, f32[1024]{0:T(1024)}, f32[1024]{0:T(1024)}, f32[1024]{0:T(1024)}) all-reduce(f32[]{:T(128)} %get-tuple-element.1256, f32[1024]{0:T(1024)S(1)} %get-tuple-element.1254, f32[1024]{0:T(1024)S(1)} %copy-done.87, f32[1024]{0:T(1024)S(1)} %copy-done.72), channel_id=1, replica_groups=mesh['row'=4,'col'=8] {'row','col'}, use_global_device_ids=true, to_apply=%region_15.16 | all-reduce | flops 3073 | bytes 24584 | tf_op jit(solution)/shard_map/psum | solution.py:483
  (633 shorter events, 264.8 us)
Async XLA Ops:
  7.2 348.7 %copy-start = (bf16[128,4096]{1,0:T(8,128)(2,1)S(1)}, bf16[128,4096]{1,0:T(8,128)(2,1)}, u32[]{:S(2)}) copy-start(bf16[128,4096]{1,0:T(8,128)(2,1)} %param.39) | copy-start | bytes 3145732
  7.2 38.9 %copy-start.78 = (bf16[128,256]{1,0:T(8,128)(2,1)S(1)}, bf16[128,256]{1,0:T(8,128)(2,1)}, u32[]{:S(2)}) copy-start(bf16[128,256]{1,0:T(8,128)(2,1)} %param.41) | copy-start | bytes 196612
  7.2 231.1 %all-gather.9.cloned.1.call-start = ((), (), s32[]{:S(2)}) async-start(), calls=%async_computation.14 | async-start | bytes 2621440 | tf_op jit(solution)/shard_map/all_gather | solution.py:196
  11.2 68.4 %copy-start.79 = (bf16[128,256]{1,0:T(8,128)(2,1)S(1)}, bf16[128,256]{1,0:T(8,128)(2,1)}, u32[]{:S(2)}) copy-start(bf16[128,256]{1,0:T(8,128)(2,1)} %param.36) | copy-start | bytes 196612
  11.3 237.9 %all-gather.11.cloned.1.call-start = ((), (), s32[]{:S(2)}) async-start(), calls=%async_computation.15 | async-start | bytes 2359296 | tf_op jit(solution)/shard_map/all_gather | solution.py:176
  46.1 65.9 %copy-start.80 = (bf16[128,256]{1,0:T(8,128)(2,1)S(1)}, bf16[128,256]{1,0:T(8,128)(2,1)}, u32[]{:S(2)}) copy-start(bf16[128,256]{1,0:T(8,128)(2,1)} %param.37) | copy-start | bytes 196612
  78.7 64.8 %copy-start.81 = (bf16[128,256]{1,0:T(8,128)(2,1)S(1)}, bf16[128,256]{1,0:T(8,128)(2,1)}, u32[]{:S(2)}) copy-start(bf16[128,256]{1,0:T(8,128)(2,1)} %param.42) | copy-start | bytes 196612
  111.9 64.2 %copy-start.82 = (bf16[128,256]{1,0:T(8,128)(2,1)S(1)}, bf16[128,256]{1,0:T(8,128)(2,1)}, u32[]{:S(2)}) copy-start(bf16[128,256]{1,0:T(8,128)(2,1)} %param.43) | copy-start | bytes 196612
  143.5 64.9 %copy-start.44 = (bf16[1,512,1024]{2,1,0:T(8,128)(2,1)S(1)}, bf16[1,512,1024]{2,1,0:T(8,128)(2,1)}, u32[]{:S(2)}) copy-start(bf16[1,512,1024]{2,1,0:T(8,128)(2,1)} %param.29) | copy-start | bytes 3145732
  143.5 94.8 %copy-start.69 = (bf16[1024,768]{1,0:T(8,128)(2,1)}, bf16[1024,768]{1,0:T(8,128)(2,1)S(1)}, u32[]{:S(2)}) copy-start(bf16[1024,768]{1,0:T(8,128)(2,1)S(1)} %constant_dynamic-update-slice_fusion.3) | copy-start | bytes 4718596
  143.6 65.1 %copy-start.83 = (bf16[256,128]{1,0:T(8,128)(2,1)S(1)}, bf16[256,128]{1,0:T(8,128)(2,1)}, u32[]{:S(2)}) copy-start(bf16[256,128]{1,0:T(8,128)(2,1)} %param.38) | copy-start | bytes 196612
  249.2 27.0 %all-gather.23.cloned.1.call-start = ((), (), s32[]{:S(2)}) async-start(), calls=%async_computation.35 | async-start | bytes 1310720 | tf_op jit(solution)/shard_map/while/body/eval_jaxpr/all_gather | solution.py:228
  281.4 27.7 %all-gather.23.cloned.1.call-start = ((), (), s32[]{:S(2)}) async-start(), calls=%async_computation.35 | async-start | bytes 1310720 | tf_op jit(solution)/shard_map/while/body/eval_jaxpr/all_gather | solution.py:228
  314.3 73.0 %reduce-scatter.21.cloned.1.call-start = ((), (), s32[]{:S(2)}) async-start(), calls=%async_computation.16 | async-start | bytes 2621440 | tf_op jit(solution)/shard_map/reduce_scatter | solution.py:267
  355.7 31.6 %copy-start.17 = (bf16[1,256,1024]{2,1,0:T(8,128)(2,1)S(1)}, bf16[1,256,1024]{2,1,0:T(8,128)(2,1)}, u32[]{:S(2)}) copy-start(bf16[1,256,1024]{2,1,0:T(8,128)(2,1)} %param.28) | copy-start | bytes 1572868
  355.7 32.9 %copy-start.85 = (f32[1024]{0:T(1024)S(1)}, f32[1024]{0:T(1024)}, u32[]{:S(2)}) copy-start(f32[1024]{0:T(1024)} %param.46) | copy-start | bytes 12292
  355.8 83.7 %all-gather.15.cloned.1.call-start = ((), (), s32[]{:S(2)}) async-start(), calls=%async_computation.18 | async-start | bytes 2359296 | tf_op jit(solution)/shard_map/all_gather | solution.py:171
  356.6 106.1 %all-gather.13.cloned.1.call-start = ((), (), s32[]{:S(2)}) async-start(), calls=%async_computation.17 | async-start | bytes 2621440 | tf_op jit(solution)/shard_map/all_gather | solution.py:276
  390.7 126.0 %all-gather.17.cloned.1.call-start = ((), (), s32[]{:S(2)}) async-start(), calls=%async_computation.19 | async-start | bytes 2359296 | tf_op jit(solution)/shard_map/all_gather | solution.py:172
  392.5 160.8 %reduce-scatter.23.cloned.1.call-start = ((), (), s32[]{:S(2)}) async-start(), calls=%async_computation.20 | async-start | bytes 2621440 | tf_op jit(solution)/shard_map/reduce_scatter | solution.py:279
  523.5 29.8 %copy-start.30 = (bf16[256,1024]{1,0:T(8,128)(2,1)S(1)}, bf16[256,1024]{1,0:T(8,128)(2,1)}, u32[]{:S(2)}) copy-start(bf16[256,1024]{1,0:T(8,128)(2,1)} %reduce-scatter.21.cloned.1.call-done) | copy-start | bytes 1572868
  523.5 29.8 %copy-start.42 = (bf16[1,256,1024]{2,1,0:T(8,128)(2,1)S(1)}, bf16[1,256,1024]{2,1,0:T(8,128)(2,1)}, u32[]{:S(2)}) copy-start(bf16[1,256,1024]{2,1,0:T(8,128)(2,1)} %param.30) | copy-start | bytes 1572868
  523.5 54.7 %all-gather.19.cloned.1.call-start = ((), (), s32[]{:S(2)}) async-start(), calls=%async_computation.21 | async-start | bytes 2621440 | tf_op jit(solution)/shard_map/all_gather | solution.py:288
  555.4 67.5 %reduce-scatter.25.cloned.1.call-start = ((), (), s32[]{:S(2)}) async-start(), calls=%async_computation.22 | async-start | bytes 2621440 | tf_op jit(solution)/shard_map/reduce_scatter | solution.py:293
  591.4 31.6 %copy-start.43 = (bf16[256,1024]{1,0:T(8,128)(2,1)S(1)}, bf16[256,1024]{1,0:T(8,128)(2,1)}, u32[]{:S(2)}) copy-start(bf16[256,1024]{1,0:T(8,128)(2,1)} %reduce-scatter.23.cloned.1.call-done) | copy-start | bytes 1572868
  591.4 58.6 %all-gather.21.cloned.1.call-start = ((), (), s32[]{:S(2)}) async-start(), calls=%async_computation.23 | async-start | bytes 2621440 | tf_op jit(solution)/shard_map/all_gather | solution.py:301
  655.1 57.4 %copy-start.53 = (f32[1024]{0:T(1024)S(1)}, f32[1024]{0:T(1024)}, u32[]{:S(2)}) copy-start(f32[1024]{0:T(1024)} %param.47) | copy-start | bytes 12292
  655.1 57.4 %copy-start.55 = (f32[1024]{0:T(1024)S(1)}, f32[1024]{0:T(1024)}, u32[]{:S(2)}) copy-start(f32[1024]{0:T(1024)} %param.34) | copy-start | bytes 12292
  712.7 57.7 %all-reduce.12.cloned.1.call-start = ((), (), s32[]{:S(2)}) async-start(), calls=%async_computation.36 | async-start | bytes 2097152 | tf_op jit(solution)/shard_map/while/body/eval_jaxpr/psum | solution.py:391
  776.7 58.0 %all-reduce.12.cloned.1.call-start = ((), (), s32[]{:S(2)}) async-start(), calls=%async_computation.36 | async-start | bytes 2097152 | tf_op jit(solution)/shard_map/while/body/eval_jaxpr/psum | solution.py:391
  840.9 72.9 %reduce-scatter.45.cloned.1.call-start = ((), (), s32[]{:S(2)}) async-start(), calls=%async_computation.33 | async-start | bytes 2359296
  841.4 143.0 %reduce-scatter.35.cloned.1.call-start = ((), (), s32[]{:S(2)}) async-start(), calls=%async_computation.28 | async-start | bytes 2359296 | tf_op jit(solution)/shard_map/reduce_scatter | solution.py:456
  847.8 201.2 %reduce-scatter.43.cloned.1.call-start = ((), (), s32[]{:S(2)}) async-start(), calls=%async_computation.32 | async-start | bytes 589824
  854.0 259.1 %reduce-scatter.47.cloned.1.call-start = ((), (), s32[]{:S(2)}) async-start(), calls=%async_computation.34 | async-start | bytes 589824
  855.2 322.6 %reduce-scatter.29.cloned.1.call-start = ((), (), s32[]{:S(2)}) async-start(), calls=%async_computation.25 | async-start | bytes 589824 | tf_op jit(solution)/shard_map/reduce_scatter | solution.py:438
  863.6 378.4 %reduce-scatter.31.cloned.1.call-start = ((), (), s32[]{:S(2)}) async-start(), calls=%async_computation.26 | async-start | bytes 589824 | tf_op jit(solution)/shard_map/reduce_scatter | solution.py:441
  864.2 443.1 %reduce-scatter.33.cloned.1.call-start = ((), (), s32[]{:S(2)}) async-start(), calls=%async_computation.27 | async-start | bytes 589824 | tf_op jit(solution)/shard_map/reduce_scatter | solution.py:447
  864.9 506.7 %reduce-scatter.37.cloned.1.call-start = ((), (), s32[]{:S(2)}) async-start(), calls=%async_computation.29 | async-start | bytes 589824 | tf_op jit(solution)/shard_map/reduce_scatter | solution.py:462
  868.4 567.9 %reduce-scatter.39.cloned.1.call-start = ((), (), s32[]{:S(2)}) async-start(), calls=%async_computation.30 | async-start | bytes 589824 | tf_op jit(solution)/shard_map/reduce_scatter | solution.py:465
  869.1 631.3 %reduce-scatter.41.cloned.1.call-start = ((), (), s32[]{:S(2)}) async-start(), calls=%async_computation.31 | async-start | bytes 589824 | tf_op jit(solution)/shard_map/reduce_scatter | solution.py:471
  869.7 663.8 %reduce-scatter.27.cloned.1.call-start = ((), (), s32[]{:S(2)}) async-start(), calls=%async_computation.24 | async-start | bytes 2621440 | tf_op jit(solution)/shard_map/reduce_scatter | solution.py:429
  874.3 659.2 %copy-start.18 = (bf16[1,256,1024]{2,1,0:T(8,128)(2,1)S(1)}, bf16[1,256,1024]{2,1,0:T(8,128)(2,1)}, u32[]{:S(2)}) copy-start(bf16[1,256,1024]{2,1,0:T(8,128)(2,1)} %param.28) | copy-start | bytes 1572868
  874.3 659.2 %copy-start.86 = (f32[1024]{0:T(1024)S(1)}, f32[1024]{0:T(1024)}, u32[]{:S(2)}) copy-start(f32[1024]{0:T(1024)} %param.45) | copy-start | bytes 12292
  874.3 659.2 %copy-start.89 = (f32[256]{0:T(256)S(1)}, f32[256]{0:T(256)}, u32[]{:S(2)}) copy-start(f32[256]{0:T(256)} %copy-done.88) | copy-start | bytes 3076
  914.9 620.2 %copy-start.72 = (f32[1024]{0:T(1024)S(1)}, f32[1024]{0:T(1024)}, u32[]{:S(2)}) copy-start(f32[1024]{0:T(1024)} %get-tuple-element.864) | copy-start | bytes 12292
  914.9 620.2 %copy-start.87 = (f32[1024]{0:T(1024)S(1)}, f32[1024]{0:T(1024)}, u32[]{:S(2)}) copy-start(f32[1024]{0:T(1024)} %get-tuple-element.1252) | copy-start | bytes 12292
  914.9 660.5 %copy-start.45 = (f32[256,1024]{1,0:T(8,128)S(1)}, f32[256,1024]{1,0:T(8,128)}, u32[]{:S(2)}) copy-start(f32[256,1024]{1,0:T(8,128)} %get-tuple-element.1392) | copy-start | bytes 3145732
  1500.4 77.4 %copy-start.1 = (bf16[128,4096]{1,0:T(8,128)(2,1)S(1)}, bf16[128,4096]{1,0:T(8,128)(2,1)}, u32[]{:S(2)}) copy-start(bf16[128,4096]{1,0:T(8,128)(2,1)} %param.39) | copy-start | bytes 3145732
  (130 other events, 387.5 us)
Sparse Core Ops, SparseCore 0:
  11.4 25.2 all-gather.8
  38.7 59.5 all-gather.10
  260.1 15.9 all-gather.22
  292.3 16.7 all-gather.22
  355.9 31.4 reduce-scatter.20
  390.1 49.2 all-gather.14
  441.6 21.0 all-gather.12
  465.6 51.0 all-gather.16
  523.7 29.5 reduce-scatter.22
  555.6 22.5 all-gather.18
  591.5 31.3 reduce-scatter.24
  627.4 22.6 all-gather.20
  734.3 36.0 all-reduce.11
  798.2 36.4 all-reduce.11
  845.3 68.4 reduce-scatter.44
  917.6 66.8 reduce-scatter.34
  988.0 60.9 reduce-scatter.42
  1052.2 60.9 reduce-scatter.46
  1116.9 60.9 reduce-scatter.28
  1181.0 60.9 reduce-scatter.30
  1246.3 60.9 reduce-scatter.32
  1310.6 60.9 reduce-scatter.36
  1375.3 60.9 reduce-scatter.38
  1439.4 60.8 reduce-scatter.40
  1503.1 30.4 reduce-scatter.26
where the time goes:
time: 1600 us; the launch traced here: 1590 us
  waiting for transfers between devices  970 us (61%)
  blocking collectives  260 us (16%)
  matrix products  144 us (9%)
  local copies, waits for them, and re-layouts  112 us (7%)
  other arithmetic  73.3 us (5%)
  between operations  18.4 us (1%)
    unnamed x24, waiting for transfers between devices  168 us
    reduce_scatter x1, waiting for transfers between devices, per_device(): lax.psum_scatter(upper_grad.astype(jnp.bfloat16), 'col', scatter_dimensio...  68.7 us
    reduce_scatter x1, waiting for transfers between devices, per_device(): lax.psum_scatter(token_grad[:, 2 * local_width:].astype(jnp.bfloat16), 'c...  63.7 us
    reduce_scatter x1, waiting for transfers between devices, per_device(): lax.psum_scatter(trio_grad[:, local_width:2 * local_width].astype(jnp.bfl...  63.2 us
    reduce_scatter x1, waiting for transfers between devices, per_device(): lax.psum_scatter(token_grad[:, :local_width].astype(jnp.bfloat16), 'col',...  63 us
    reduce_scatter x1, waiting for transfers between devices, per_device(): lax.psum_scatter(trio_grad[:, :local_width].astype(jnp.bfloat16), 'col',...  62.8 us
    reduce_scatter x1, waiting for transfers between devices, per_device(): lax.psum_scatter(token_grad[:, local_width:2 * local_width].astype(jnp.bf...  62.7 us
    reduce_scatter x1, waiting for transfers between devices, per_device(): lax.psum_scatter(trio_grad[:, 2 * local_width:].astype(jnp.bfloat16), 'co...  62.6 us
  transfers between devices with their start and end apart: 25, of which 23 were waited for; matrix products, arithmetic and copies ran while one was open for 7% of the time, Pallas kernels for 0%

commit v1 on v0

v1 whole, which is shorter than its diff:
```python
import functools

import jax
import jax.numpy as jnp
from jax import lax
from jax.experimental import pallas as pl
from jax.experimental.pallas import tpu as pltpu
from jax.sharding import PartitionSpec as P

HEAD = 128
BLOCK = 512
HALF = 256
NS = 512
PIECE = 256

epsilon = 1e-06
masked_value = -1e30
score_scale = HEAD ** (-0.5)
log2_scale = score_scale * 1.4426950408889634
f32 = jnp.float32
bf16 = jnp.bfloat16


def dot_nn(a, b):
    return lax.dot_general(a, b, (((1,), (0,)), ((), ())), preferred_element_type=f32)


def dot_nt(a, b):
    return lax.dot_general(a, b, (((1,), (1,)), ((), ())), preferred_element_type=f32)


def dot_tn(a, b):
    return lax.dot_general(a, b, (((0,), (0,)), ((), ())), preferred_element_type=f32)


def half_of(i, s):
    return lax.rem(i + 1 + s[1], 2)


def launch(body, grid, idx, inputs, outputs, scratch=(), flops=0, vmem=40, name=None):
    arrays = [a for a, unused in inputs]
    nbytes = sum(a.size * a.dtype.itemsize for a in arrays)
    nbytes += sum(o.size * o.dtype.itemsize for o, unused in outputs)
    return pl.pallas_call(
        body,
        grid_spec=pltpu.PrefetchScalarGridSpec(
            num_scalar_prefetch=1,
            grid=grid,
            in_specs=[spec for unused, spec in inputs],
            out_specs=[spec for unused, spec in outputs],
            scratch_shapes=list(scratch),
        ),
        out_shape=[o for o, unused in outputs],
        compiler_params=pltpu.CompilerParams(
            dimension_semantics=("arbitrary",) * len(grid), vmem_limit_bytes=vmem << 20
        ),
        cost_estimate=pl.CostEstimate(flops=flops, bytes_accessed=nbytes, transcendentals=0),
        name=name,
    )(idx, *arrays)


def shaped(shape, dtype):
    return jax.ShapeDtypeStruct(shape, dtype)


def whole(shape, place=(0, 0)):
    return pl.BlockSpec(shape, lambda i, s: place, pipeline_mode=pl.Buffered(1))


def norm_project(idx, values, gain, weights, column, width, name):
    rows, features = values.shape

    def body(s, x_ref, g_ref, w_ref, n_ref, p_ref):
        x = x_ref[...].astype(f32)
        inverse = lax.rsqrt(jnp.mean(x * x, axis=-1, keepdims=True) + epsilon)
        normed = (x * inverse * g_ref[...]).astype(bf16)
        n_ref[...] = normed
        p_ref[...] = dot_nn(normed, w_ref[...]).astype(bf16)

    return launch(
        body,
        (rows // HALF,),
        idx,
        [
            (values, pl.BlockSpec((HALF, features), lambda i, s: (i, 0))),
            (gain, whole((1, features))),
            (weights, whole((features, width), (0, column))),
        ],
        [
            (shaped((rows, features), bf16), pl.BlockSpec((HALF, features), lambda i, s: (i, 0))),
            (shaped((rows, width), bf16), pl.BlockSpec((HALF, width), lambda i, s: (i, 0))),
        ],
        flops=2 * rows * features * width,
        name=name,
    )


def masked_scores(kind, keys, queries, katt, qatt):
    scores = dot_nt(keys, queries)
    if kind == "free":
        return scores
    if kind == "valid":
        return jnp.where(katt[:, 2:3] > 0, scores, masked_value)
    places = lax.broadcasted_iota(jnp.int32, scores.shape, 0)
    asking = lax.broadcasted_iota(jnp.int32, scores.shape, 1)
    same = katt[:, 0:1] == qatt[0:1, :]
    if kind == "prev":
        allowed = same & (places > asking)
    else:
        allowed = same & ((places <= asking) | (katt[:, 1:2] == qatt[1:2, :]))
    return jnp.where(allowed, scores, masked_value)


def attention_inputs(queries, segments, katt, qatt):
    q_arr, q_row, q_col = queries
    inputs = [(q_arr, pl.BlockSpec((BLOCK, HEAD), lambda h, s: (q_row, q_col + h)))]
    for kind, k_arr, row, k_col, v_col, att in segments:
        inputs.append(
            (k_arr, pl.BlockSpec((BLOCK, HEAD), lambda h, s, row=row, k_col=k_col: (row, k_col + h)))
        )
        inputs.append(
            (k_arr, pl.BlockSpec((BLOCK, HEAD), lambda h, s, row=row, v_col=v_col: (row, v_col + h)))
        )
        if att is not None:
            inputs.append((katt, pl.BlockSpec((BLOCK, 4), lambda h, s, att=att: (att, 0))))
    if qatt is not None:
        inputs.append((qatt, pl.BlockSpec((4, BLOCK), lambda h, s: (0, q_row))))
    return inputs


def take_attention(refs, segments, has_qatt):
    refs = list(refs)
    q = refs.pop(0)[...]
    parts = []
    for kind, unused_a, unused_b, unused_c, unused_d, att in segments:
        k = refs.pop(0)[...]
        v = refs.pop(0)[...]
        katt = refs.pop(0)[...] if att is not None else None
        parts.append((kind, k, v, katt))
    qatt = refs.pop(0)[...] if has_qatt else None
    return q, parts, qatt, refs


def attend(idx, queries, segments, katt, qatt, heads, name):
    inputs = attention_inputs(queries, segments, katt, qatt)

    def body(s, *refs):
        q, parts, qa, rest = take_attention(refs, segments, qatt is not None)
        o_ref, l_ref = rest
        scores = [masked_scores(kind, k, q, ka, qa) for kind, k, v, ka in parts]
        largest = functools.reduce(
            jnp.maximum, [jnp.max(x, axis=0, keepdims=True) for x in scores]
        )
        total = jnp.zeros_like(largest)
        mixed = jnp.zeros((HEAD, BLOCK), f32)
        for x, (kind, k, v, ka) in zip(scores, parts):
            raised = jnp.exp2((x - largest) * log2_scale)
            total = total + jnp.sum(raised, axis=0, keepdims=True)
            mixed = mixed + dot_tn(v, raised.astype(bf16))
        o_ref[...] = jnp.transpose(mixed * (1.0 / total)).astype(bf16)
        l_ref[0] = largest * log2_scale + jnp.log2(total)

    keys = BLOCK * len(segments)
    return launch(
        body,
        (heads,),
        idx,
        inputs,
        [
            (shaped((BLOCK, heads * HEAD), bf16), pl.BlockSpec((BLOCK, HEAD), lambda h, s: (0, h))),
            (shaped((heads, 1, BLOCK), f32), pl.BlockSpec((1, 1, BLOCK), lambda h, s: (h, 0, 0))),
        ],
        flops=4 * heads * BLOCK * keys * HEAD * 2,
        name=name,
    )


def attend_back(idx, queries, segments, katt, qatt, heads, logs, upstream, added, dtypes, name):
    inputs = attention_inputs(queries, segments, katt, qatt)
    inputs.append((logs, pl.BlockSpec((1, 1, BLOCK), lambda h, s: (h, 0, 0))))
    by_head = pl.BlockSpec((BLOCK, HEAD), lambda h, s: (0, h))
    inputs.append((upstream, by_head))
    for pair in added:
        if pair is not None:
            inputs.extend([(pair[0], by_head), (pair[1], by_head)])
    outputs = [(shaped((BLOCK, heads * HEAD), bf16), by_head)]
    for dtype in dtypes:
        outputs.extend([(shaped((BLOCK, heads * HEAD), dtype), by_head)] * 2)

    def body(s, *refs):
        q, parts, qa, rest = take_attention(refs, segments, qatt is not None)
        log_total = rest.pop(0)[0]
        go = rest.pop(0)[...]
        sums = []
        for pair in added:
            sums.append((rest.pop(0), rest.pop(0)) if pair is not None else None)
        gq_ref = rest.pop(0)
        chances, grads = [], []
        inner = jnp.zeros((1, BLOCK), f32)
        for kind, k, v, ka in parts:
            x = masked_scores(kind, k, q, ka, qa)
            chance = jnp.exp2(x * log2_scale - log_total)
            grad = dot_nt(v, go)
            inner = inner + jnp.sum(chance * grad, axis=0, keepdims=True)
            chances.append(chance)
            grads.append(grad)
        gq = jnp.zeros((HEAD, BLOCK), f32)
        for (kind, k, v, ka), chance, grad, pair, dtype in zip(parts, chances, grads, sums, dtypes):
            gl = (chance * (grad - inner)).astype(bf16)
            gk = dot_nn(gl, q) * score_scale
            gv = dot_nn(chance.astype(bf16), go)
            gq = gq + dot_tn(k, gl)
            if pair is not None:
                gk = gk + pair[0][...]
                gv = gv + pair[1][...]
            gk_ref, gv_ref = rest.pop(0), rest.pop(0)
            gk_ref[...] = gk.astype(dtype)
            gv_ref[...] = gv.astype(dtype)
        gq_ref[...] = jnp.transpose(gq * score_scale).astype(bf16)

    keys = BLOCK * len(segments)
    return launch(
        body,
        (heads,),
        idx,
        inputs,
        outputs,
        flops=10 * heads * BLOCK * keys * HEAD * 2,
        name=name,
    )


def state_update(idx, pieces, write_t, column, state, retain, gain, weights, w_col, width, name):
    rows, features = state.shape
    count, piece_width = len(pieces), pieces[0].shape[1]
    project = weights is not None

    def body(s, *refs):
        refs = list(refs)
        piece_refs = [refs.pop(0) for unused in range(count)]
        w_ref, s_ref, r_ref = refs[:3]
        refs = refs[3:]
        scr = refs.pop()
        for k, ref in enumerate(piece_refs):
            scr[s[0] ^ k] = ref[...]
        update = jnp.zeros((HALF, features), f32)
        for k in range(count):
            update = update + dot_nt(scr[k], w_ref[:, k * piece_width : (k + 1) * piece_width])
        keep = r_ref[...]
        following = keep * s_ref[...].astype(f32) + (1.0 - keep) * update
        if project:
            g_ref, p_ref, out_ref, n_ref, t_ref = refs
            inverse = lax.rsqrt(jnp.mean(following * following, axis=-1, keepdims=True) + epsilon)
            normed = (following * inverse * g_ref[...]).astype(bf16)
            n_ref[...] = normed
            t_ref[...] = dot_nn(normed, p_ref[...]).astype(bf16)
        else:
            (out_ref,) = refs
        out_ref[...] = following

    tile = lambda w: pl.BlockSpec((HALF, w), lambda i, s: (i, 0))
    inputs = [(p, tile(piece_width)) for p in pieces]
    inputs += [
        (write_t, whole((features, features), (0, column))),
        (state, tile(features)),
        (retain, whole((1, features))),
    ]
    outputs = [(shaped((rows, features), f32), tile(features))]
    if project:
        inputs += [(gain, whole((1, features))), (weights, whole((features, width), (0, w_col)))]
        outputs += [
            (shaped((rows, features), bf16), tile(features)),
            (shaped((rows, width), bf16), tile(width)),
        ]
    return launch(
        body,
        (rows // HALF,),
        idx,
        inputs,
        outputs,
        scratch=[pltpu.VMEM((count, HALF, piece_width), bf16)],
        flops=2 * rows * features * (features + (width if project else 0)),
        name=name,
    )


def take_sum(i, refs, total):
    mine, mine_other, theirs, theirs_other = refs

    @pl.when(i == 0)
    def _():
        total[...] = theirs[...].astype(f32) + theirs_other[...].astype(f32)

    @pl.when(i == 1)
    def _():
        total[...] = mine[...].astype(f32) + mine_other[...].astype(f32)

    return total[...]


def sum_inputs(sums):
    return [(a, whole(a.shape)) for a in sums]


def halves(features, row_block=0):
    return pl.BlockSpec((HALF, features), lambda i, s: (2 * row_block + half_of(i, s), 0))


def fixed(shape):
    return pl.BlockSpec(shape, lambda i, s: (0, 0))


def add_rows(i, ref, value):
    value = jnp.sum(value, axis=0, keepdims=True)

    @pl.when(i == 0)
    def _():
        ref[...] = value

    @pl.when(i != 0)
    def _():
        ref[...] = ref[...] + value


def put_half(i, theirs_ref, mine_ref, value):
    @pl.when(i == 0)
    def _():
        theirs_ref[...] = value

    @pl.when(i == 1)
    def _():
        mine_ref[...] = value


def project_back(idx, grads, weights, column, name):
    rows, width = grads[0].shape
    features = weights.shape[0]

    def body(s, *refs):
        i = pl.program_id(0)
        *g_refs, w_ref, theirs_ref, mine_ref = refs
        out = jnp.zeros((HALF, features), f32)
        for k, ref in enumerate(g_refs):
            out = out + dot_nt(ref[...], w_ref[:, k * width : (k + 1) * width])
        put_half(i, theirs_ref, mine_ref, out.astype(bf16))

    return launch(
        body,
        (2,),
        idx,
        [(g, halves(width)) for g in grads]
        + [(weights, whole((features, len(grads) * width), (0, column)))],
        [(shaped((HALF, features), bf16), fixed((HALF, features)))] * 2,
        flops=2 * rows * features * width * len(grads),
        name=name,
    )


def state_back(idx, sums, state, following, retain, gain, write_t, w_col, width, name):
    rows, features = state.shape
    before = write_t is not None

    def body(s, *refs):
        i = pl.program_id(0)
        refs = list(refs)
        total = refs.pop()
        up = take_sum(i, [refs.pop(0) for unused in range(4)], total)
        s_ref, r_ref, g_ref = refs[:3]
        refs = refs[3:]
        x = s_ref[...].astype(f32)
        inverse = lax.rsqrt(jnp.mean(x * x, axis=-1, keepdims=True) + epsilon)
        unit = x * inverse
        scaled = up * g_ref[...]
        inner = jnp.mean(scaled * unit, axis=-1, keepdims=True)
        out = inverse * (scaled - unit * inner)
        if following is not None:
            out = r_ref[...] * refs.pop(0)[...] + out
        if before:
            w_ref, gs_ref, gain_ref, gu_ref, gos_ref = refs
            gu = ((1.0 - r_ref[...]) * out).astype(bf16)
            gu_ref[...] = gu
            gos_ref[...] = dot_nn(gu, w_ref[...]).astype(bf16)
        else:
            gs_ref, gain_ref = refs
        gs_ref[...] = out
        add_rows(i, gain_ref, up * unit)

    inputs = sum_inputs(sums) + [
        (state, halves(features)),
        (retain, whole((1, features))),
        (gain, whole((1, features))),
    ]
    outputs = [
        (shaped((rows, features), f32), halves(features)),
        (shaped((1, features), f32), fixed((1, features))),
    ]
    if following is not None:
        inputs.append((following, halves(features)))
    if before:
        inputs.append(
            (
                write_t,
                pl.BlockSpec(
                    (features, width),
                    lambda i, s: (0, w_col + s[2]),
                    pipeline_mode=pl.Buffered(1),
                ),
            )
        )
        outputs += [
            (shaped((rows, features), bf16), halves(features)),
            (shaped((rows, width), bf16), halves(width)),
        ]
    return launch(
        body,
        (2,),
        idx,
        inputs,
        outputs,
        scratch=[pltpu.VMEM((HALF, features), f32)],
        flops=2 * rows * features * width if before else rows * features * 10,
        name=name,
    )


def gelu_both(a):
    root, cubic = 0.7978845608028654, 0.044715
    squared = a * a
    bent = jnp.tanh(root * (a + cubic * (squared * a)))
    rising = 0.5 * (1.0 + bent)
    slope = rising + (0.5 * root) * a * (1.0 - bent * bent) * (1.0 + (3.0 * cubic) * squared)
    return a * rising, slope


def dense_forward(idx, number, pieces, out_pieces, tokens, gain, dense, name):
    features = tokens.shape[1]
    hidden = features_of_hidden = dense[2]
    weights, modelt_col = dense[0], dense[1]
    count, width = len(pieces), pieces[0].shape[1]

    def body(s, *refs):
        i = pl.program_id(0)
        refs = list(refs)
        o_refs = [refs.pop(0) for unused in range(count)]
        w_refs = [refs.pop(0) for unused in range(count)]
        t_ref, g_ref, up_ref, down_ref = refs[:4]
        x1_ref, xn_ref, h_ref, d_ref, theirs_ref, mine_ref = refs[4:]
        x1 = t_ref[...].astype(f32)
        for o_ref, w_ref in zip(o_refs, w_refs):
            x1 = x1 + dot_nt(o_ref[...], w_ref[...])
        x1_ref[...] = x1
        inverse = lax.rsqrt(jnp.mean(x1 * x1, axis=-1, keepdims=True) + epsilon)
        normed = (x1 * inverse * g_ref[...]).astype(bf16)
        xn_ref[...] = normed
        h, slope = gelu_both(dot_nn(normed, up_ref[...]))
        h = h.astype(bf16)
        h_ref[...] = h
        d_ref[...] = slope.astype(bf16)
        put_half(i, theirs_ref, mine_ref, dot_nt(h, down_ref[...]).astype(bf16))

    return launch(
        body,
        (2,),
        idx,
        [(p, halves(width)) for p in pieces]
        + [(w, whole((features, width))) for w in out_pieces]
        + [
            (tokens, halves(features, number)),
            (gain, whole((1, features))),
            (weights, whole((features, hidden), (0, 0))),
            (weights, whole((features, hidden), (0, modelt_col))),
        ],
        [
            (shaped((BLOCK, features), f32), halves(features)),
            (shaped((BLOCK, features), bf16), halves(features)),
            (shaped((BLOCK, hidden), bf16), halves(hidden)),
            (shaped((BLOCK, hidden), bf16), halves(hidden)),
            (shaped((HALF, features), bf16), fixed((HALF, features))),
            (shaped((HALF, features), bf16), fixed((HALF, features))),
        ],
        flops=2 * BLOCK * features * (features + 2 * hidden),
        name=name,
    )


def dense_backward(idx, number, sums, x1, teacher, weight_of_row, slope, dense, name):
    features = x1.shape[1]
    weights, modelt_col, hidden = dense

    def body(s, *refs):
        i = pl.program_id(0)
        refs = list(refs)
        total = refs.pop()
        dense_sum = take_sum(i, [refs.pop(0) for unused in range(4)], total)
        x_ref, t_ref, v_ref, d_ref, up_ref, down_ref = refs[:6]
        gy_ref, gm_ref, ga_ref, loss_ref, theirs_ref, mine_ref = refs[6:]
        errors = x_ref[...] + dense_sum - t_ref[...].astype(f32)
        gy = v_ref[...] * errors
        gy_ref[...] = gy
        add_rows(i, loss_ref, gy * errors)
        gm = gy.astype(bf16)
        gm_ref[...] = gm
        ga = (dot_nn(gm, down_ref[...]) * d_ref[...].astype(f32)).astype(bf16)
        ga_ref[...] = ga
        put_half(i, theirs_ref, mine_ref, dot_nt(ga, up_ref[...]).astype(bf16))

    return launch(
        body,
        (2,),
        idx,
        sum_inputs(sums)
        + [
            (x1, halves(features)),
            (teacher, halves(features, number)),
            (weight_of_row, halves(1, number)),
            (slope, halves(hidden)),
            (weights, whole((features, hidden), (0, 0))),
            (weights, whole((features, hidden), (0, modelt_col))),
        ],
        [
            (shaped((BLOCK, features), f32), halves(features)),
            (shaped((BLOCK, features), bf16), halves(features)),
            (shaped((BLOCK, hidden), bf16), halves(hidden)),
            (shaped((1, features), f32), fixed((1, features))),
            (shaped((HALF, features), bf16), fixed((HALF, features))),
            (shaped((HALF, features), bf16), fixed((HALF, features))),
        ],
        scratch=[pltpu.VMEM((HALF, features), f32)],
        flops=4 * BLOCK * features * hidden,
        name=name,
    )


def output_backward(idx, sums, gy, x1, gain, out_own, name):
    features = x1.shape[1]
    width = out_own.shape[1]

    def body(s, *refs):
        i = pl.program_id(0)
        refs = list(refs)
        total = refs.pop()
        up = take_sum(i, [refs.pop(0) for unused in range(4)], total)
        gy_ref, x_ref, g_ref, w_ref, gx_ref, gp_ref, go_ref, gain_ref = refs
        x = x_ref[...]
        inverse = lax.rsqrt(jnp.mean(x * x, axis=-1, keepdims=True) + epsilon)
        unit = x * inverse
        scaled = up * g_ref[...]
        inner = jnp.mean(scaled * unit, axis=-1, keepdims=True)
        gx = gy_ref[...] + inverse * (scaled - unit * inner)
        gx_ref[...] = gx
        gp = gx.astype(bf16)
        gp_ref[...] = gp
        go_ref[...] = dot_nn(gp, w_ref[...]).astype(bf16)
        add_rows(i, gain_ref, up * unit)

    return launch(
        body,
        (2,),
        idx,
        sum_inputs(sums)
        + [
            (gy, halves(features)),
            (x1, halves(features)),
            (gain, whole((1, features))),
            (out_own, whole((features, width))),
        ],
        [
            (shaped((BLOCK, features), f32), halves(features)),
            (shaped((BLOCK, features), bf16), halves(features)),
            (shaped((BLOCK, width), bf16), halves(width)),
            (shaped((1, features), f32), fixed((1, features))),
        ],
        scratch=[pltpu.VMEM((HALF, features), f32)],
        flops=2 * BLOCK * features * width,
        name=name,
    )


def weight_grads(idx, groups, name):
    features = groups[0][0][0].shape[1]
    inputs, total = [], 0
    flops = 0
    for parts in groups:
        for left, right in parts:
            inputs.append((left, pl.BlockSpec((left.shape[0], HALF), lambda i, s: (0, i))))
            inputs.append((right, whole(right.shape)))
            flops += 2 * left.size * right.shape[1]
        total += parts[0][1].shape[1]

    def body(s, *refs):
        refs = list(refs)
        out_ref = refs.pop()
        at = 0
        for parts in groups:
            size = parts[0][1].shape[1]
            out = jnp.zeros((HALF, size), f32)
            for unused in parts:
                left, right = refs.pop(0), refs.pop(0)
                out = out + dot_tn(left[...], right[...])
            out_ref[:, at : at + size] = out.astype(bf16)
            at += size

    return launch(
        body,
        (features // HALF,),
        idx,
        inputs,
        [(shaped((features, total), bf16), pl.BlockSpec((HALF, total), lambda i, s: (i, 0)))],
        flops=flops,
        name=name,
    )[0]


def per_device(
    block_input,
    state_start,
    teacher,
    valid_mask,
    segment,
    image_offset,
    retain,
    to_query,
    to_key,
    to_value,
    to_output,
    to_hidden,
    to_model,
    state_query,
    state_key,
    state_value,
    state_write,
    first_gain,
    second_gain,
    state_gain,
):
    row_devices = lax.axis_size("row")
    col_devices = lax.axis_size("col")
    row_index = lax.axis_index("row")
    col_index = lax.axis_index("col")
    local_rows, features = block_input.shape[1:]
    length = local_rows * row_devices
    width = to_query.shape[1]
    heads = width // HEAD
    hidden = to_hidden.shape[1] // row_devices
    nblocks = length // BLOCK
    pairs = row_devices == 4 and 2 * local_rows == BLOCK
    core_pairs = [(k, k ^ 1) for k in range(row_devices)]
    chip_pairs = [(k, k ^ 2) for k in range(row_devices)] if pairs else None
    if pairs:
        idx = jnp.stack([row_index, row_index % 2, row_index]).astype(jnp.int32)
    else:
        idx = jnp.stack([0, 1, row_index]).astype(jnp.int32)

    def to_core(x):
        return lax.ppermute(x, "row", core_pairs)

    def to_chip(x):
        return lax.ppermute(x, "row", chip_pairs)

    def row_pieces(x):
        if not pairs:
            stacked = lax.all_gather(x, "row", axis=0, tiled=False)
            return [stacked[k] for k in range(row_devices)]
        near = to_core(x)
        far = to_chip(x)
        return [x, near, far, to_core(far)]

    def row_order(x):
        if not pairs:
            return lax.all_gather(x, "row", axis=0, tiled=True)
        out = jnp.zeros((row_devices,) + x.shape, x.dtype)
        for k, piece in enumerate(row_pieces(x)):
            out = lax.dynamic_update_index_in_dim(out, piece, row_index ^ k, 0)
        return out.reshape((-1,) + x.shape[1:])

    def chip_sum(theirs, mine):
        return (mine.astype(f32) + to_core(theirs).astype(f32)).astype(bf16)

    def row_sum(theirs, mine):
        if not pairs:
            both = lax.psum(jnp.concatenate([theirs, mine]), "row")
            none = jnp.zeros_like(mine)
            return [both[HALF:], none, both[:HALF], none]
        own = chip_sum(theirs, mine)
        far = to_chip(own)
        return [own, far, to_core(own), to_core(far)]

    def all_sum(x):
        for axis, size in (("row", row_devices), ("col", col_devices)):
            step = 1
            while step < size:
                x = x + lax.ppermute(x, axis, [(k, k ^ step) for k in range(size)])
                step *= 2
        return x

    near_weights = jnp.concatenate(
        [state_query, state_key, state_value, to_query, to_key, to_value], axis=1
    )
    near = lax.all_gather(near_weights, "col", axis=0, tiled=True)
    upper = lax.dynamic_slice_in_dim(to_hidden, row_index * hidden, hidden, 1)
    lower = lax.dynamic_slice_in_dim(to_model, row_index * hidden, hidden, 0)
    mid = lax.all_gather(
        jnp.concatenate([state_write.T, to_output.T], axis=1), "col", axis=0, tiled=True
    )
    far = lax.all_gather(jnp.concatenate([upper, lower.T], axis=1), "col", axis=0, tiled=True)
    dense = (far, 1, hidden)
    out_own = lax.slice_in_dim(mid, features, features + width, axis=1)
    out_pieces = row_pieces(out_own)

    valid_row = lax.dynamic_index_in_dim(valid_mask, col_index, 0, keepdims=False)
    segment_row = segment[0]
    numbers = jnp.arange(nblocks, dtype=jnp.int32)
    places = jnp.arange(length, dtype=jnp.int32)
    starts = numbers * BLOCK + image_offset[0]
    inside = (places[:, None] >= starts[None, :]) & (places[:, None] < starts[None, :] + PIECE)
    piece = jnp.sum(jnp.where(inside, numbers[None, :] + 1, 0), axis=1) - 1
    nothing = jnp.zeros_like(piece)
    katt = jnp.stack(
        [jnp.where(valid_row > 0, segment_row, -1), piece, valid_row, nothing], axis=1
    )
    qatt = jnp.stack([segment_row, jnp.where(piece >= 0, piece, -2), nothing, nothing], axis=0)
    valid_count = jnp.sum(valid_mask.astype(f32))
    total_tokens = f32(length * col_devices)
    weight_of_row = (total_tokens / valid_count * valid_row.astype(f32))[:, None]
    retain2 = retain[None]
    first_gain2, second_gain2, state_gain2 = first_gain[None], second_gain[None], state_gain[None]

    tokens = row_order(block_input[0])
    teacher_all = row_order(teacher[0])
    first_low, token_heads = norm_project(idx, tokens, first_gain2, near, 1, 3 * width, "token_proj")

    def token_segments(number, trio):
        found = []
        if number > 0:
            found.append(("prev", token_heads, number - 1, heads, 2 * heads, number - 1))
        found.append(("own", token_heads, number, heads, 2 * heads, number))
        found.append(("free", trio, 0, heads, 2 * heads, None))
        return found

    def state_segments(number, trio):
        return [
            ("valid", token_heads, number, heads, 2 * heads, number),
            ("free", trio, 0, heads, 2 * heads, None),
        ]

    current = state_start[0]
    state_low, trio = norm_project(idx, current, state_gain2, near, 0, 3 * width, "state_proj")
    states, lows, trios = [], [], []
    state_out, state_logs, token_out, token_logs = [], [], [], []
    x1s, second_lows, hiddens, slopes, dense_sums = [], [], [], [], []
    for b in range(nblocks):
        states.append(current)
        lows.append(state_low)
        trios.append(trio)
        mixed, logs = attend(
            idx, (trio, 0, 0), state_segments(b, trio), katt, None, heads, f"state_attend{b}"
        )
        state_out.append(mixed)
        state_logs.append(logs)
        pieces = row_pieces(mixed)
        mixed, logs = attend(
            idx, (token_heads, b, 0), token_segments(b, trio), katt, qatt, heads, f"token_attend{b}"
        )
        token_out.append(mixed)
        token_logs.append(logs)
        if b + 1 < nblocks:
            current, state_low, trio = state_update(
                idx, pieces, mid, 0, current, retain2, state_gain2, near, 0, 3 * width, f"update{b}"
            )
        else:
            (final_state,) = state_update(
                idx, pieces, mid, 0, current, retain2, None, None, 0, 0, f"update{b}"
            )
        x1, low, h, slope, theirs, mine = dense_forward(
            idx, b, row_pieces(mixed), out_pieces, tokens, second_gain2, dense, f"dense{b}"
        )
        x1s.append(x1)
        second_lows.append(low)
        hiddens.append(h)
        slopes.append(slope)
        dense_sums.append(row_sum(theirs, mine))

    gms, gas, losses, gx1s, gps, gos, second_sums = [], [], [], [], [], [], []
    for b in range(nblocks):
        gy, gm, ga, loss, theirs, mine = dense_backward(
            idx, b, dense_sums[b], x1s[b], teacher_all, weight_of_row, slopes[b], dense, f"back{b}"
        )
        gms.append(gm)
        gas.append(ga)
        losses.append(loss)
        gx1, gp, go, gain_sum = output_backward(
            idx, row_sum(theirs, mine), gy, x1s[b], second_gain2, out_own, f"out_back{b}"
        )
        gx1s.append(gx1)
        gps.append(gp)
        gos.append(go)
        second_sums.append(gain_sum)
    dense_grads = weight_grads(
        idx,
        [list(zip(second_lows, gas)), list(zip(gms, hiddens))],
        "dense_grads",
    )
    dense_grads = lax.psum_scatter(dense_grads, "col", scatter_dimension=0, tiled=True)

    grad_next = None
    key_part = None
    gain_sums = []
    gus = [None] * nblocks
    trio_grads = [None] * nblocks
    token_grads = [None] * nblocks
    first_halves = [None] * nblocks
    gu = ((1.0 - retain2) * jnp.zeros((NS, features), f32)).astype(bf16)
    write_own = lax.dynamic_slice_in_dim(mid, row_index * width, width, 1)
    gos_state = dot_nn(gu, write_own).astype(bf16)
    for b in reversed(range(nblocks)):
        gus[b] = gu
        last = b + 1 == nblocks

        def token_part(own, free, dtype):
            segments = token_segments(b, trios[b])
            added = ([None] if b > 0 else []) + [own, free]
            dtypes = ([f32] if b > 0 else []) + [dtype, dtype]
            return attend_back(
                idx,
                (token_heads, b, 0),
                segments,
                katt,
                qatt,
                heads,
                token_logs[b],
                gos[b],
                added,
                dtypes,
                f"token_back{b}",
            )

        def state_part(own, free, dtype):
            return attend_back(
                idx,
                (trios[b], 0, 0),
                state_segments(b, trios[b]),
                katt,
                None,
                heads,
                state_logs[b],
                gos_state,
                [own, free],
                [dtype, dtype],
                f"state_back{b}",
            )

        if last:
            gqs, gk, gv, gks, gvs = state_part(key_part, None, f32)
            found = token_part((gk, gv), (gks, gvs), bf16)
            gq, (gk, gv, gks, gvs) = found[0], found[-4:]
        else:
            found = token_part(key_part, None, f32)
            gq, (gk, gv, gks, gvs) = found[0], found[-4:]
            gqs, gk, gv, gks, gvs = state_part((gk, gv), (gks, gvs), bf16)
        key_part = (found[1], found[2]) if b > 0 else None
        trio_grads[b] = (gqs, gks, gvs)
        token_grads[b] = (gq, gk, gv)
        theirs, mine = project_back(idx, trio_grads[b], near, 0, f"trio_back{b}")
        sums = row_sum(theirs, mine)
        first_halves[b] = project_back(idx, token_grads[b], near, 1, f"first_back{b}")
        if b > 0:
            grad_next, gain_sum, gu, gos_state = state_back(
                idx,
                sums,
                states[b],
                grad_next,
                retain2,
                state_gain2,
                mid,
                0,
                width,
                f"chain_back{b}",
            )
        else:
            grad_next, gain_sum = state_back(
                idx, sums, states[b], grad_next, retain2, state_gain2, None, 0, width, "chain_back0"
            )
        gain_sums.append(gain_sum)

    late_grads = weight_grads(
        idx,
        [[(lows[b], trio_grads[b][k]) for b in range(nblocks)] for k in range(3)]
        + [
            [
                (lax.slice_in_dim(first_low, b * BLOCK, (b + 1) * BLOCK), token_grads[b][k])
                for b in range(nblocks)
            ]
            for k in range(3)
        ]
        + [list(zip(gps, token_out)), list(zip(gus, state_out))],
        "late_grads",
    )
    late_grads = lax.psum_scatter(late_grads, "col", scatter_dimension=0, tiled=True)

    if pairs:
        own_rows, arrived = [], []
        for b in range(nblocks):
            own = chip_sum(*first_halves[b])
            own_rows.append(own)
            senders = [(k, k ^ 2) for k in range(row_devices) if k // 2 != b]
            arrived.append(lax.ppermute(own, "row", senders))
        mine_first = row_index // 2 == 0
        grad_first = jnp.where(mine_first, own_rows[0], own_rows[1]).astype(f32) + jnp.where(
            mine_first, arrived[0], arrived[1]
        ).astype(f32)
        own_gx1 = jnp.where(mine_first, gx1s[0], gx1s[1])
        own_gx1 = lax.dynamic_slice_in_dim(own_gx1, row_index % 2 * HALF, HALF)
    else:
        both = jnp.concatenate([half for pair in first_halves for half in pair])
        grad_first = lax.psum_scatter(both, "row", scatter_dimension=0, tiled=True).astype(f32)
        own_gx1 = lax.dynamic_slice_in_dim(
            jnp.concatenate(gx1s), row_index * local_rows, local_rows
        )
    own_tokens = block_input[0].astype(f32)
    inverse = lax.rsqrt(jnp.mean(own_tokens * own_tokens, axis=-1, keepdims=True) + epsilon)
    unit = own_tokens * inverse
    scaled = grad_first * first_gain2
    inner = jnp.mean(scaled * unit, axis=-1, keepdims=True)
    input_grad = own_gx1 + inverse * (scaled - unit * inner)
    first_sum = jnp.sum(grad_first * unit, axis=0)

    share = 1.0 / row_devices
    summed = all_sum(
        jnp.stack(
            [
                sum(losses)[0] * share,
                first_sum,
                sum(second_sums)[0] * share,
                sum(gain_sums)[0] * share,
            ]
        )
    )
    total_loss = jnp.sum(summed[0]) / (2.0 * total_tokens)

    dense_grads = dense_grads.astype(f32)
    late = late_grads.astype(f32)

    def part(k):
        return lax.slice_in_dim(late, k * width, (k + 1) * width, axis=1)

    return (
        total_loss,
        final_state[None],
        input_grad[None],
        grad_next[None],
        part(3),
        part(4),
        part(5),
        part(6).T,
        dense_grads[:, :hidden],
        dense_grads[:, hidden:].T,
        part(0),
        part(1),
        part(2),
        part(7).T,
        summed[1],
        summed[2],
        summed[3],
    )


def solution(mesh):
    in_specs = (
        P("col", "row", None),
        P("col", None, None),
        P("col", "row", None),
        P(),
        P("col", None),
        P("col", None),
        P(),
        P("col", "row"),
        P("col", "row"),
        P("col", "row"),
        P("row", "col"),
        P("col", None),
        P(None, "col"),
        P("col", "row"),
        P("col", "row"),
        P("col", "row"),
        P(None, "col"),
        P(),
        P(),
        P(),
    )
    out_specs = (
        P(),
        P("col", None, None),
        P("col", "row", None),
        P("col", None, None),
        P("col", "row"),
        P("col", "row"),
        P("col", "row"),
        P("row", "col"),
        P("col", "row"),
        P("row", "col"),
        P("col", "row"),
        P("col", "row"),
        P("col", "row"),
        P("row", "col"),
        P(),
        P(),
        P(),
    )
    return jax.shard_map(
        per_device, mesh=mesh, in_specs=in_specs, out_specs=out_specs, check_vma=False
    )
```

time: 1600 us -> 526 us (0.33)
  waiting for transfers between devices: 970 us -> 243 us
  blocking collectives: 260 us -> 0 us
  matrix products: 144 us -> 1.49 us
  Pallas kernels: 0 us -> 121 us
  other arithmetic: 73.3 us -> 17.4 us
  starting transfers between devices: 1.76 us -> 32.6 us
  local copies, waits for them, and re-layouts: 112 us -> 82.9 us
    reduce_scatter x11 -> x2, waiting for transfers between devices: 568 us -> 9.41 us  [the longest x1 9.39 us: per_device(): lax.psum_scatter(late_grads, 'col', scatter_dimension=0, tiled=True)]
    all_gather x7 -> x0, blocking collectives: 221 us -> none  [the longest x1 33.1 us: per_device(): lax.all_gather(to_query, 'col', axis=0, tiled=True)]
    unnamed x24 -> x5, waiting for transfers between devices: 168 us -> 0.08 us
    dot_general x52 -> x1, matrix products: 144 us -> 1.49 us  [dot_nn(): lax.dot_general(a, b, (((1,), (0,)), ((), ())), preferred_element_type=f32)]
    pallas_call x0 -> x26, Pallas kernels: none -> 121 us  [launch(): pl.pallas_call(body, grid_spec=pltpu.PrefetchScalarGridSpec(num_scalar_pr...]
    ppermute x0 -> x54, waiting for transfers between devices: none -> 116 us  [the longest x13 101 us: to_chip(): return lax.ppermute(x, 'row', chip_pairs)]
    all_gather x9 -> x3, waiting for transfers between devices: 178 us -> 117 us  [the longest x1 58.5 us: per_device(): near = lax.all_gather(near_weights, 'col', axis=0, tiled=True)]
    psum x2 -> x0, waiting for transfers between devices: 55.7 us -> none  [chain_back(): lax.psum(grad_normed.astype(jnp.bfloat16), 'row').astype(jnp.float32)]
  transfers between devices with their start and end apart: 25 -> 59, of which waited for: 23 -> 21; matrix products, arithmetic and copies ran while one was open for 7% -> 7% of each run, Pallas kernels for 0% -> 21%
where the time goes in v1:
time: 526 us; the launch traced here: 516 us
  waiting for transfers between devices  243 us (46%)
  Pallas kernels  121 us (23%)
  local copies, waits for them, and re-layouts  82.9 us (16%)
  starting transfers between devices  32.6 us (6%)
  between operations  18 us (3%)
  other arithmetic  17.4 us (3%)
    pallas_call x26, Pallas kernels, launch(): pl.pallas_call(body, grid_spec=pltpu.PrefetchScalarGridSpec(num_scalar_pr...  121 us
    ppermute x13, waiting for transfers between devices, to_chip(): return lax.ppermute(x, 'row', chip_pairs)  101 us
    unnamed x265, local copies, waits for them, and re-layouts  69.2 us
    all_gather x1, waiting for transfers between devices, per_device(): near = lax.all_gather(near_weights, 'col', axis=0, tiled=True)  58.5 us
    all_gather x1, waiting for transfers between devices, per_device(): lax.all_gather(jnp.concatenate([state_write.T, to_output.T], axis=1), 'co...  30.7 us
    all_gather x1, waiting for transfers between devices, per_device(): lax.all_gather(jnp.concatenate([upper, lower.T], axis=1), 'col', axis=0,...  27.4 us
    ppermute x13, starting transfers between devices, to_chip(): return lax.ppermute(x, 'row', chip_pairs)  17.4 us
  transfers between devices with their start and end apart: 59, of which 21 were waited for; matrix products, arithmetic and copies ran while one was open for 7% of the time, Pallas kernels for 21%

profile of v1, /device:TPU:0, one launch (start us, length us, event | category | flops | bytes accessed | tf_op | source)
XLA Modules:
  0.0 516.0 jit_solution(6700694356578586590)
XLA Ops:
  17.2 2.6 collective-permute-start.1
  20.3 12.1 %collective-permute-done.1 = bf16[256,1024]{1,0:T(8,128)(2,1)} collective-permute-done((bf16[256,1024]{1,0:T(8,128)(2,1)S(1)}, bf16[256,1024]{1,0:T(8,128)(2,1)}, u32[]{:S(2)}, u32[]{:S(2)}) %collective-permute-start.1) | collective-permute-done | bytes 524320 | tf_op jit(solution)/shard_map/ppermute | solution.py:658
  37.5 30.7 %all-gather.6.cloned.1.call-done.refs_4_.refs_7_ = bf16[1024,1280]{1,0:T(8,128)(2,1)} async-done(((bf16[128,1280]{1,0:T(8,128)(2,1)}), bf16[1024,1280]{1,0:T(8,128)(2,1)}) %all-gather.6.cloned.1.call-update) | async-done | bytes 2621456 | tf_op jit(solution)/shard_map/all_gather | solution.py:702
  71.5 58.5 %all-gather.4.cloned.1.call-done.w_ref.refs_8_.refs_3_ = bf16[1024,1536]{1,0:T(8,128)(2,1)} async-done(((bf16[128,1536]{1,0:T(8,128)(2,1)}), bf16[1024,1536]{1,0:T(8,128)(2,1)}) %all-gather.4.cloned.1.call-update) | async-done | bytes 3145744 | tf_op jit(solution)/shard_map/all_gather | solution.py:699
  133.1 2.1 state_proj.1
  137.9 3.5 token_proj.1
  141.4 3.2 state_attend0.1
  146.2 5.6 %collective-permute-done.17.refs_2_ = bf16[512,256]{1,0:T(8,128)(2,1)S(1)} collective-permute-done((bf16[512,256]{1,0:T(8,128)(2,1)S(1)}, bf16[512,256]{1,0:T(8,128)(2,1)S(1)}, u32[]{:S(2)}, u32[]{:S(2)}) %collective-permute-start.17) | collective-permute-done | bytes 262176 | tf_op jit(solution)/shard_map/ppermute | solution.py:658
  152.6 3.3 token_attend0.1
  157.4 4.1 update0.1
  161.6 4.7 token_attend1.1
  169.0 6.0 %collective-permute-done.20.refs_2_ = bf16[512,256]{1,0:T(8,128)(2,1)} collective-permute-done((bf16[512,256]{1,0:T(8,128)(2,1)}, bf16[512,256]{1,0:T(8,128)(2,1)}, u32[]{:S(2)}, u32[]{:S(2)}) %collective-permute-start.20) | collective-permute-done | bytes 262176 | tf_op jit(solution)/shard_map/ppermute | solution.py:658
  177.2 27.4 %all-gather.8.cloned.1.call-done.refs_10_.refs_11_.refs_8_.refs_9_ = bf16[1024,2048]{1,0:T(8,128)(2,1)} async-done(((bf16[128,2048]{1,0:T(8,128)(2,1)}), bf16[1024,2048]{1,0:T(8,128)(2,1)}) %all-gather.8.cloned.1.call-update) | async-done | bytes 4194320 | tf_op jit(solution)/shard_map/all_gather | solution.py:705
  212.1 9.3 %dense0.1 = (f32[512,1024]{1,0:T(8,128)S(1)}, bf16[512,1024]{1,0:T(8,128)(2,1)S(1)}, bf16[512,1024]{1,0:T(8,128)(2,1)S(1)}, bf16[512,1024]{1,0:T(8,128)(2,1)S(1)...) custom-call(s32[3]{0:T(128)S(1)} %pad_add_fusion.1.s, bf16[512,256]{1,0:T(8,128)(2,1)S(1)} %copy-done.45, ...), custom_call_target="tpu_custom_call" | custom-call | flops 3221225472 | bytes 19927040 | tf_op jit(solution)/shard_map/dense0/pallas_call | solution.py:44
  226.4 9.8 %dense1.1 = (f32[512,1024]{1,0:T(8,128)S(1)}, bf16[512,1024]{1,0:T(8,128)(2,1)S(1)}, bf16[512,1024]{1,0:T(8,128)(2,1)S(1)}, bf16[512,1024]{1,0:T(8,128)(2,1)S(1)...) custom-call(s32[3]{0:T(128)S(1)} %pad_add_fusion.1.s, bf16[512,256]{1,0:T(8,128)(2,1)} %get-tuple-element.110.refs_0_.refs_27_, ...), custom_call_target="tpu_custom_call" | custom-call | flops 3221225472 | bytes 19927040 | tf_op jit(solution)/shard_map/dense1/pallas_call | solution.py:44
  250.3 6.5 %collective-permute-done.14 = bf16[256,1024]{1,0:T(8,128)(2,1)} collective-permute-done((bf16[256,1024]{1,0:T(8,128)(2,1)}, bf16[256,1024]{1,0:T(8,128)(2,1)}, u32[]{:S(2)}, u32[]{:S(2)}) %collective-permute-start.14) | collective-permute-done | bytes 524320 | tf_op jit(solution)/shard_map/ppermute | solution.py:658
  258.9 9.0 %collective-permute-done.10.refs_1_ = bf16[256,1024]{1,0:T(8,128)(2,1)S(1)} collective-permute-done((bf16[256,1024]{1,0:T(8,128)(2,1)S(1)}, bf16[256,1024]{1,0:T(8,128)(2,1)S(1)}, u32[]{:S(2)}, u32[]{:S(2)}) %collective-permute-start.10) | collective-permute-done | bytes 524320 | tf_op jit(solution)/shard_map/ppermute | solution.py:658
  269.6 8.6 %collective-permute-done.23.refs_1_ = bf16[256,1024]{1,0:T(8,128)(2,1)S(1)} collective-permute-done((bf16[256,1024]{1,0:T(8,128)(2,1)S(1)}, bf16[256,1024]{1,0:T(8,128)(2,1)S(1)}, u32[]{:S(2)}, u32[]{:S(2)}) %collective-permute-start.23) | collective-permute-done | bytes 524320 | tf_op jit(solution)/shard_map/ppermute | solution.py:658
  279.5 6.7 %back0.1 = (f32[512,1024]{1,0:T(8,128)S(1)}, bf16[512,1024]{1,0:T(8,128)(2,1)S(1)}, bf16[512,1024]{1,0:T(8,128)(2,1)S(1)}, f32[1,1024]{1,0:T(1,128)S(1)}, bf16[2...) custom-call(s32[3]{0:T(128)S(1)} %pad_add_fusion.1.s, bf16[256,1024]{1,0:T(8,128)(2,1)S(1)} %add_convert_fusion.7.refs_0_, ...), custom_call_target="tpu_custom_call" | custom-call | flops 2147483648 | bytes 20979712 | tf_op jit(solution)/shard_map/back0/pallas_call | solution.py:44
  289.4 7.2 %back1.1 = (f32[512,1024]{1,0:T(8,128)S(1)}, bf16[512,1024]{1,0:T(8,128)(2,1)S(1)}, bf16[512,1024]{1,0:T(8,128)(2,1)S(1)}, f32[1,1024]{1,0:T(1,128)S(1)}, bf16[2...) custom-call(s32[3]{0:T(128)S(1)} %pad_add_fusion.1.s, bf16[256,1024]{1,0:T(8,128)(2,1)S(1)} %add_convert_fusion.6.refs_0_, ...), custom_call_target="tpu_custom_call" | custom-call | flops 2147483648 | bytes 20979712 | tf_op jit(solution)/shard_map/back1/pallas_call | solution.py:44
  307.7 6.3 %dense_grads.1 = bf16[1024,2048]{1,0:T(8,128)(2,1)S(1)} custom-call(s32[3]{0:T(128)S(1)} %pad_add_fusion.1.s, bf16[512,1024]{1,0:T(8,128)(2,1)S(1)} %copy-done.95, bf16[512,1024]{1,0:T(8,128)(2,1)S(1)} %copy-done.105, bf16[512,1024]{1,0:T(8,128)(2,1)S(1)} %copy-done.99, bf16[512,1024]{1,0:T(8,128)(2,1)S(1)} %copy-done.109, ...), custom_call_target="tpu_custom_call" | custom-call | flops 4294967296 | bytes 12582912 | tf_op jit(solution)/shard_map/dense_grads/pallas_call | solution.py:44
  318.3 2.0 add_convert_fusion.4.refs_0_
  321.6 13.2 %collective-permute-done.31.refs_1_ = bf16[256,1024]{1,0:T(8,128)(2,1)} collective-permute-done((bf16[256,1024]{1,0:T(8,128)(2,1)}, bf16[256,1024]{1,0:T(8,128)(2,1)}, u32[]{:S(2)}, u32[]{:S(2)}) %collective-permute-start.31) | collective-permute-done | bytes 524320 | tf_op jit(solution)/shard_map/ppermute | solution.py:658
  336.4 3.6 state_attend1.1
  340.1 4.8 state_back1.1
  345.5 3.7 out_back1.1
  350.6 6.4 %token_back1.1 = (bf16[512,256]{1,0:T(8,128)(2,1)S(1)}, f32[512,256]{1,0:T(8,128)S(1)}, f32[512,256]{1,0:T(8,128)S(1)}, bf16[512,256]{1,0:T(8,128)(2,1)S(1)}, bf...) custom-call(s32[3]{0:T(128)S(1)} %pad_add_fusion.1.s, ...), custom_call_target="tpu_custom_call" | custom-call | flops 4026531840 | bytes 14209024 | tf_op jit(solution)/shard_map/token_back1/pallas_call | solution.py:44
  357.0 2.0 trio_back1.1
  362.4 11.7 %collective-permute-done.27.refs_1_ = bf16[256,1024]{1,0:T(8,128)(2,1)S(1)} collective-permute-done((bf16[256,1024]{1,0:T(8,128)(2,1)S(1)}, bf16[256,1024]{1,0:T(8,128)(2,1)S(1)}, u32[]{:S(2)}, u32[]{:S(2)}) %collective-permute-start.27) | collective-permute-done | bytes 524320 | tf_op jit(solution)/shard_map/ppermute | solution.py:658
  374.6 10.3 %collective-permute-done.35.refs_1_ = bf16[256,1024]{1,0:T(8,128)(2,1)S(1)} collective-permute-done((bf16[256,1024]{1,0:T(8,128)(2,1)S(1)}, bf16[256,1024]{1,0:T(8,128)(2,1)S(1)}, u32[]{:S(2)}, u32[]{:S(2)}) %collective-permute-start.35) | collective-permute-done | bytes 524320 | tf_op jit(solution)/shard_map/ppermute | solution.py:658
  387.2 3.3 out_back0.1
  391.9 5.0 token_back0.1
  397.0 2.5 chain_back1.1
  400.8 4.9 state_back0.1
  406.7 9.7 %late_grads.1 = bf16[1024,2048]{1,0:T(8,128)(2,1)} custom-call(s32[3]{0:T(128)S(1)} %pad_add_fusion.1.s, bf16[512,1024]{1,0:T(8,128)(2,1)S(1)} %copy-done.16, bf16[512,256]{1,0:T(8,128)(2,1)S(1)} %get-tuple-element.158.refs_0_.refs_1_, bf16[512,1024]{1,0:T(8,128)(2,1)S(1)} %copy-done.18, bf16[512,256]{1,0:T(8,128)(2,1)S(1)} %get-tuple-element.135.refs_0_.refs_3_, ...), custom_call_target="tpu_custom_call" | custom-call | flops 4294967296 | bytes 25165824 | tf_op jit(solution)/shard_map/late_grads/pallas_call | solution.py:44
  421.0 2.8 first_back1.1
  424.3 2.8 trio_back0.1
  429.8 2.0 first_back0.1
  433.7 3.2 collective-permute-start.41
  440.3 2.7 collective-permute-start.52
  443.0 17.4 %collective-permute-done.43.refs_1_ = bf16[256,1024]{1,0:T(8,128)(2,1)S(1)} collective-permute-done((bf16[256,1024]{1,0:T(8,128)(2,1)S(1)}, bf16[256,1024]{1,0:T(8,128)(2,1)S(1)}, u32[]{:S(2)}, u32[]{:S(2)}) %collective-permute-start.43) | collective-permute-done | bytes 524320 | tf_op jit(solution)/shard_map/ppermute | solution.py:658
  460.4 3.9 collective-permute-done.40
  465.8 3.1 chain_back0.1
  470.4 3.7 collective-permute-done.47
  476.4 4.2 update1.1
  481.6 2.9 collective-permute-done.49
  487.5 2.5 collective-permute-done.50
  495.0 9.4 %reduce-scatter.3.cloned.1.call-done = bf16[128,2048]{1,0:T(8,128)(2,1)} async-done(((bf16[1024,2048]{1,0:T(8,128)(2,1)}), bf16[128,2048]{1,0:T(8,128)(2,1)}) %reduce-scatter.3.cloned.1.call-update) | async-done | bytes 524304 | tf_op jit(solution)/shard_map/reduce_scatter | solution.py:898
  (430 shorter events, 126.8 us)
Async XLA Ops:
  7.2 61.0 %all-gather.6.cloned.1.call-start = ((), (), s32[]{:S(2)}) async-start(), calls=%async_computation.3 | async-start | bytes 2949120 | tf_op jit(solution)/shard_map/all_gather | solution.py:702
  10.2 119.9 %all-gather.4.cloned.1.call-start = ((), (), s32[]{:S(2)}) async-start(), calls=%async_computation.2 | async-start | bytes 3538944 | tf_op jit(solution)/shard_map/all_gather | solution.py:699
  14.5 190.1 %all-gather.8.cloned.1.call-start = ((), (), s32[]{:S(2)}) async-start(), calls=%async_computation.4 | async-start | bytes 4718592 | tf_op jit(solution)/shard_map/all_gather | solution.py:705
  16.6 475.3 %reduce-scatter.5.cloned.1.call-start = ((), (), s32[]{:S(2)}) async-start(), calls=%async_computation.6 | async-start | bytes 4718592 | tf_op jit(solution)/shard_map/reduce_scatter | solution.py:803
  16.7 16.1 %collective-permute-start = (bf16[256,1024]{1,0:T(8,128)(2,1)S(1)}, bf16[256,1024]{1,0:T(8,128)(2,1)}, u32[]{:S(2)}, u32[]{:S(2)}) collective-permute-start(bf16[256,1024]{1,0:T(8,128)(2,1)S(1)} %bitcast.76), channel_id=1, source_target_pairs={{0,8},{8,0},{16,24},{24,16},{1,9},{9,1},{17,25},{25,17},{2,10},{10... | collective-permute-start | bytes 1572872 | tf_op jit(solution)/shard_map/ppermute | solution.py:655
  17.2 15.2 %collective-permute-start.1 = (bf16[256,1024]{1,0:T(8,128)(2,1)S(1)}, bf16[256,1024]{1,0:T(8,128)(2,1)}, u32[]{:S(2)}, u32[]{:S(2)}) collective-permute-start(bf16[256,1024]{1,0:T(8,128)(2,1)S(1)} %bitcast.77), channel_id=1, source_target_pairs={{0,16},{8,24},{16,0},{24,8},{1,17},{9,25},{17,1},{25,9},{2,18},{10... | collective-permute-start | bytes 1572872 | tf_op jit(solution)/shard_map/ppermute | solution.py:658
  70.1 82.4 %collective-permute-start.7 = (bf16[1024,256]{1,0:T(8,128)(2,1)}, bf16[1024,256]{1,0:T(8,128)(2,1)}, u32[]{:S(2)}, u32[]{:S(2)}) collective-permute-start(bf16[1024,256]{1,0:T(8,128)(2,1)} %slice.72.refs_4_.refs_7_), channel_id=1, source_target_pairs={{0,16},{8,24},{16,0},{24,8},{1,17},{9,25},{17,1},{25,9},{2,18},{10... | collective-permute-start | bytes 1572872 | tf_op jit(solution)/shard_map/ppermute | solution.py:658
  144.6 7.3 %collective-permute-start.17 = (bf16[512,256]{1,0:T(8,128)(2,1)S(1)}, bf16[512,256]{1,0:T(8,128)(2,1)S(1)}, u32[]{:S(2)}, u32[]{:S(2)}) collective-permute-start(bf16[512,256]{1,0:T(8,128)(2,1)S(1)} %get-tuple-element.108.refs_0_.refs_29_), channel_id=1, source_target_pairs={{0,16},{8,24},{16,0},{24,8},{1,17},{9,25},{17,1},{25,9},{2,18},{10... | collective-permute-start | bytes 786440 | tf_op jit(solution)/shard_map/ppermute | solution.py:658
  146.2 11.2 %collective-permute-start.16 = (bf16[512,256]{1,0:T(8,128)(2,1)S(1)}, bf16[512,256]{1,0:T(8,128)(2,1)S(1)}, u32[]{:S(2)}, u32[]{:S(2)}) collective-permute-start(bf16[512,256]{1,0:T(8,128)(2,1)S(1)} %get-tuple-element.108.refs_0_.refs_29_), channel_id=1, source_target_pairs={{0,8},{8,0},{16,24},{24,16},{1,9},{9,1},{17,25},{25,17},{2,10},{10... | collective-permute-start | bytes 786440 | tf_op jit(solution)/shard_map/ppermute | solution.py:655
  151.9 16.2 %collective-permute-start.6 = (bf16[1024,256]{1,0:T(8,128)(2,1)}, bf16[1024,256]{1,0:T(8,128)(2,1)S(1)}, u32[]{:S(2)}, u32[]{:S(2)}) collective-permute-start(bf16[1024,256]{1,0:T(8,128)(2,1)} %slice.72.refs_4_.refs_7_), channel_id=1, source_target_pairs={{0,8},{8,0},{16,24},{24,16},{1,9},{9,1},{17,25},{25,17},{2,10},{10... | collective-permute-start | bytes 1572872 | tf_op jit(solution)/shard_map/ppermute | solution.py:655
  152.5 22.5 %collective-permute-start.8 = (bf16[1024,256]{1,0:T(8,128)(2,1)}, bf16[1024,256]{1,0:T(8,128)(2,1)S(1)}, u32[]{:S(2)}, u32[]{:S(2)}) collective-permute-start(bf16[1024,256]{1,0:T(8,128)(2,1)} %collective-permute-done.7.refs_6_), channel_id=1, source_target_pairs={{0,8},{8,0},{16,24},{24,16},{1,9},{9,1},{17,25},{25,17},{2,10},{10... | collective-permute-start | bytes 1572872 | tf_op jit(solution)/shard_map/ppermute | solution.py:655
  155.9 11.0 %collective-permute-start.4 = (bf16[512,256]{1,0:T(8,128)(2,1)S(1)}, bf16[512,256]{1,0:T(8,128)(2,1)S(1)}, u32[]{:S(2)}, u32[]{:S(2)}) collective-permute-start(bf16[512,256]{1,0:T(8,128)(2,1)S(1)} %get-tuple-element.102.refs_0_.refs_25_), channel_id=1, source_target_pairs={{0,16},{8,24},{16,0},{24,8},{1,17},{9,25},{17,1},{25,9},{2,18},{10... | collective-permute-start | bytes 786440 | tf_op jit(solution)/shard_map/ppermute | solution.py:658
  166.3 8.7 %collective-permute-start.20 = (bf16[512,256]{1,0:T(8,128)(2,1)}, bf16[512,256]{1,0:T(8,128)(2,1)}, u32[]{:S(2)}, u32[]{:S(2)}) collective-permute-start(bf16[512,256]{1,0:T(8,128)(2,1)} %get-tuple-element.110.refs_0_.refs_27_), channel_id=1, source_target_pairs={{0,16},{8,24},{16,0},{24,8},{1,17},{9,25},{17,1},{25,9},{2,18},{10... | collective-permute-start | bytes 786440 | tf_op jit(solution)/shard_map/ppermute | solution.py:658
  166.9 8.9 %collective-permute-start.3 = (bf16[512,256]{1,0:T(8,128)(2,1)S(1)}, bf16[512,256]{1,0:T(8,128)(2,1)S(1)}, u32[]{:S(2)}, u32[]{:S(2)}) collective-permute-start(bf16[512,256]{1,0:T(8,128)(2,1)S(1)} %get-tuple-element.102.refs_0_.refs_25_), channel_id=1, source_target_pairs={{0,8},{8,0},{16,24},{24,16},{1,9},{9,1},{17,25},{25,17},{2,10},{10... | collective-permute-start | bytes 786440 | tf_op jit(solution)/shard_map/ppermute | solution.py:655
  166.9 9.6 %collective-permute-start.5 = (bf16[512,256]{1,0:T(8,128)(2,1)S(1)}, bf16[512,256]{1,0:T(8,128)(2,1)S(1)}, u32[]{:S(2)}, u32[]{:S(2)}) collective-permute-start(bf16[512,256]{1,0:T(8,128)(2,1)S(1)} %collective-permute-done.4.refs_2_), channel_id=1, source_target_pairs={{0,8},{8,0},{16,24},{24,16},{1,9},{9,1},{17,25},{25,17},{2,10},{10... | collective-permute-start | bytes 786440 | tf_op jit(solution)/shard_map/ppermute | solution.py:655
  168.9 56.7 %collective-permute-start.19 = (bf16[512,256]{1,0:T(8,128)(2,1)}, bf16[512,256]{1,0:T(8,128)(2,1)}, u32[]{:S(2)}, u32[]{:S(2)}) collective-permute-start(bf16[512,256]{1,0:T(8,128)(2,1)} %get-tuple-element.110.refs_0_.refs_27_), channel_id=1, source_target_pairs={{0,8},{8,0},{16,24},{24,16},{1,9},{9,1},{17,25},{25,17},{2,10},{10... | collective-permute-start | bytes 786440 | tf_op jit(solution)/shard_map/ppermute | solution.py:655
  175.0 51.4 %collective-permute-start.21 = (bf16[512,256]{1,0:T(8,128)(2,1)}, bf16[512,256]{1,0:T(8,128)(2,1)}, u32[]{:S(2)}, u32[]{:S(2)}) collective-permute-start(bf16[512,256]{1,0:T(8,128)(2,1)} %collective-permute-done.20.refs_2_), channel_id=1, source_target_pairs={{0,8},{8,0},{16,24},{24,16},{1,9},{9,1},{17,25},{25,17},{2,10},{10... | collective-permute-start | bytes 786440 | tf_op jit(solution)/shard_map/ppermute | solution.py:655
  225.6 19.7 %collective-permute-start.9 = (bf16[256,1024]{1,0:T(8,128)(2,1)}, bf16[256,1024]{1,0:T(8,128)(2,1)}, u32[]{:S(2)}, u32[]{:S(2)}) collective-permute-start(bf16[256,1024]{1,0:T(8,128)(2,1)} %get-tuple-element.104), channel_id=1, source_target_pairs={{0,8},{8,0},{16,24},{24,16},{1,9},{9,1},{17,25},{25,17},{2,10},{10... | collective-permute-start | bytes 1572872 | tf_op jit(solution)/shard_map/ppermute | solution.py:655
  241.2 6.4 %collective-permute-start.22 = (bf16[256,1024]{1,0:T(8,128)(2,1)}, bf16[256,1024]{1,0:T(8,128)(2,1)}, u32[]{:S(2)}, u32[]{:S(2)}) collective-permute-start(bf16[256,1024]{1,0:T(8,128)(2,1)} %get-tuple-element.112), channel_id=1, source_target_pairs={{0,8},{8,0},{16,24},{24,16},{1,9},{9,1},{17,25},{25,17},{2,10},{10... | collective-permute-start | bytes 1572872 | tf_op jit(solution)/shard_map/ppermute | solution.py:655
  241.2 26.8 %collective-permute-start.13 = (bf16[256,1024]{1,0:T(8,128)(2,1)}, bf16[256,1024]{1,0:T(8,128)(2,1)}, u32[]{:S(2)}, u32[]{:S(2)}) collective-permute-start(bf16[256,1024]{1,0:T(8,128)(2,1)} %bitcast.20), channel_id=1, source_target_pairs={{0,8},{8,0},{16,24},{24,16},{1,9},{9,1},{17,25},{25,17},{2,10},{10... | collective-permute-start | bytes 1572872 | tf_op jit(solution)/shard_map/ppermute | solution.py:655
  241.7 15.1 %collective-permute-start.14 = (bf16[256,1024]{1,0:T(8,128)(2,1)}, bf16[256,1024]{1,0:T(8,128)(2,1)}, u32[]{:S(2)}, u32[]{:S(2)}) collective-permute-start(bf16[256,1024]{1,0:T(8,128)(2,1)} %bitcast.20), channel_id=1, source_target_pairs={{0,16},{8,24},{16,0},{24,8},{1,17},{9,25},{17,1},{25,9},{2,18},{10... | collective-permute-start | bytes 1572872 | tf_op jit(solution)/shard_map/ppermute | solution.py:658
  246.7 21.2 %collective-permute-start.10 = (bf16[256,1024]{1,0:T(8,128)(2,1)S(1)}, bf16[256,1024]{1,0:T(8,128)(2,1)S(1)}, u32[]{:S(2)}, u32[]{:S(2)}) collective-permute-start(bf16[256,1024]{1,0:T(8,128)(2,1)S(1)} %add_convert_fusion.7.refs_0_), channel_id=1, source_target_pairs={{0,16},{8,24},{16,0},{24,8},{1,17},{9,25},{17,1},{25,9},{2,18},{10... | collective-permute-start | bytes 1572872 | tf_op jit(solution)/shard_map/ppermute | solution.py:658
  249.1 29.2 %collective-permute-start.23 = (bf16[256,1024]{1,0:T(8,128)(2,1)S(1)}, bf16[256,1024]{1,0:T(8,128)(2,1)S(1)}, u32[]{:S(2)}, u32[]{:S(2)}) collective-permute-start(bf16[256,1024]{1,0:T(8,128)(2,1)S(1)} %add_convert_fusion.6.refs_0_), channel_id=1, source_target_pairs={{0,16},{8,24},{16,0},{24,8},{1,17},{9,25},{17,1},{25,9},{2,18},{10... | collective-permute-start | bytes 1572872 | tf_op jit(solution)/shard_map/ppermute | solution.py:658
  256.8 22.5 %collective-permute-start.15 = (bf16[256,1024]{1,0:T(8,128)(2,1)}, bf16[256,1024]{1,0:T(8,128)(2,1)S(1)}, u32[]{:S(2)}, u32[]{:S(2)}) collective-permute-start(bf16[256,1024]{1,0:T(8,128)(2,1)} %collective-permute-done.14), channel_id=1, source_target_pairs={{0,8},{8,0},{16,24},{24,16},{1,9},{9,1},{17,25},{25,17},{2,10},{10... | collective-permute-start | bytes 1572872 | tf_op jit(solution)/shard_map/ppermute | solution.py:655
  258.4 21.0 %collective-permute-start.11 = (bf16[256,1024]{1,0:T(8,128)(2,1)S(1)}, bf16[256,1024]{1,0:T(8,128)(2,1)S(1)}, u32[]{:S(2)}, u32[]{:S(2)}) collective-permute-start(bf16[256,1024]{1,0:T(8,128)(2,1)S(1)} %add_convert_fusion.7.refs_0_), channel_id=1, source_target_pairs={{0,8},{8,0},{16,24},{24,16},{1,9},{9,1},{17,25},{25,17},{2,10},{10... | collective-permute-start | bytes 1572872 | tf_op jit(solution)/shard_map/ppermute | solution.py:655
  268.0 11.4 %collective-permute-start.12 = (bf16[256,1024]{1,0:T(8,128)(2,1)S(1)}, bf16[256,1024]{1,0:T(8,128)(2,1)S(1)}, u32[]{:S(2)}, u32[]{:S(2)}) collective-permute-start(bf16[256,1024]{1,0:T(8,128)(2,1)S(1)} %collective-permute-done.10.refs_1_), channel_id=1, source_target_pairs={{0,8},{8,0},{16,24},{24,16},{1,9},{9,1},{17,25},{25,17},{2,10},{10... | collective-permute-start | bytes 1572872 | tf_op jit(solution)/shard_map/ppermute | solution.py:655
  269.1 20.3 %collective-permute-start.24 = (bf16[256,1024]{1,0:T(8,128)(2,1)S(1)}, bf16[256,1024]{1,0:T(8,128)(2,1)S(1)}, u32[]{:S(2)}, u32[]{:S(2)}) collective-permute-start(bf16[256,1024]{1,0:T(8,128)(2,1)S(1)} %add_convert_fusion.6.refs_0_), channel_id=1, source_target_pairs={{0,8},{8,0},{16,24},{24,16},{1,9},{9,1},{17,25},{25,17},{2,10},{10... | collective-permute-start | bytes 1572872 | tf_op jit(solution)/shard_map/ppermute | solution.py:655
  278.2 11.1 %collective-permute-start.25 = (bf16[256,1024]{1,0:T(8,128)(2,1)S(1)}, bf16[256,1024]{1,0:T(8,128)(2,1)S(1)}, u32[]{:S(2)}, u32[]{:S(2)}) collective-permute-start(bf16[256,1024]{1,0:T(8,128)(2,1)S(1)} %collective-permute-done.23.refs_1_), channel_id=1, source_target_pairs={{0,8},{8,0},{16,24},{24,16},{1,9},{9,1},{17,25},{25,17},{2,10},{10... | collective-permute-start | bytes 1572872 | tf_op jit(solution)/shard_map/ppermute | solution.py:655
  316.0 188.5 %reduce-scatter.3.cloned.1.call-start = ((), (), s32[]{:S(2)}) async-start(), calls=%async_computation.5 | async-start | bytes 4718592 | tf_op jit(solution)/shard_map/reduce_scatter | solution.py:898
  320.4 14.5 %collective-permute-start.31 = (bf16[256,1024]{1,0:T(8,128)(2,1)}, bf16[256,1024]{1,0:T(8,128)(2,1)}, u32[]{:S(2)}, u32[]{:S(2)}) collective-permute-start(bf16[256,1024]{1,0:T(8,128)(2,1)} %add_convert_fusion.4.refs_0_), channel_id=1, source_target_pairs={{0,16},{8,24},{16,0},{24,8},{1,17},{9,25},{17,1},{25,9},{2,18},{10... | collective-permute-start | bytes 1572872 | tf_op jit(solution)/shard_map/ppermute | solution.py:658
  321.6 23.9 %collective-permute-start.32 = (bf16[256,1024]{1,0:T(8,128)(2,1)}, bf16[256,1024]{1,0:T(8,128)(2,1)S(1)}, u32[]{:S(2)}, u32[]{:S(2)}) collective-permute-start(bf16[256,1024]{1,0:T(8,128)(2,1)} %add_convert_fusion.4.refs_0_), channel_id=1, source_target_pairs={{0,8},{8,0},{16,24},{24,16},{1,9},{9,1},{17,25},{25,17},{2,10},{10... | collective-permute-start | bytes 1572872 | tf_op jit(solution)/shard_map/ppermute | solution.py:655
  334.9 10.6 %collective-permute-start.33 = (bf16[256,1024]{1,0:T(8,128)(2,1)}, bf16[256,1024]{1,0:T(8,128)(2,1)S(1)}, u32[]{:S(2)}, u32[]{:S(2)}) collective-permute-start(bf16[256,1024]{1,0:T(8,128)(2,1)} %collective-permute-done.31.refs_1_), channel_id=1, source_target_pairs={{0,8},{8,0},{16,24},{24,16},{1,9},{9,1},{17,25},{25,17},{2,10},{10... | collective-permute-start | bytes 1572872 | tf_op jit(solution)/shard_map/ppermute | solution.py:655
  344.9 14.2 %collective-permute-start.26 = (bf16[256,1024]{1,0:T(8,128)(2,1)S(1)}, bf16[256,1024]{1,0:T(8,128)(2,1)S(1)}, u32[]{:S(2)}, u32[]{:S(2)}) collective-permute-start(bf16[256,1024]{1,0:T(8,128)(2,1)S(1)} %copy-done.111), channel_id=1, source_target_pairs={{0,8},{8,0},{16,24},{24,16},{1,9},{9,1},{17,25},{25,17},{2,10},{10... | collective-permute-start | bytes 1572872 | tf_op jit(solution)/shard_map/ppermute | solution.py:655
  359.3 14.8 %collective-permute-start.27 = (bf16[256,1024]{1,0:T(8,128)(2,1)S(1)}, bf16[256,1024]{1,0:T(8,128)(2,1)S(1)}, u32[]{:S(2)}, u32[]{:S(2)}) collective-permute-start(bf16[256,1024]{1,0:T(8,128)(2,1)S(1)} %add_convert_fusion.5.refs_0_), channel_id=1, source_target_pairs={{0,16},{8,24},{16,0},{24,8},{1,17},{9,25},{17,1},{25,9},{2,18},{10... | collective-permute-start | bytes 1572872 | tf_op jit(solution)/shard_map/ppermute | solution.py:658
  361.2 23.7 %collective-permute-start.35 = (bf16[256,1024]{1,0:T(8,128)(2,1)S(1)}, bf16[256,1024]{1,0:T(8,128)(2,1)S(1)}, u32[]{:S(2)}, u32[]{:S(2)}) collective-permute-start(bf16[256,1024]{1,0:T(8,128)(2,1)S(1)} %add_convert_fusion.3.refs_0_), channel_id=1, source_target_pairs={{0,16},{8,24},{16,0},{24,8},{1,17},{9,25},{17,1},{25,9},{2,18},{10... | collective-permute-start | bytes 1572872 | tf_op jit(solution)/shard_map/ppermute | solution.py:658
  362.4 22.7 %collective-permute-start.28 = (bf16[256,1024]{1,0:T(8,128)(2,1)S(1)}, bf16[256,1024]{1,0:T(8,128)(2,1)S(1)}, u32[]{:S(2)}, u32[]{:S(2)}) collective-permute-start(bf16[256,1024]{1,0:T(8,128)(2,1)S(1)} %add_convert_fusion.5.refs_0_), channel_id=1, source_target_pairs={{0,8},{8,0},{16,24},{24,16},{1,9},{9,1},{17,25},{25,17},{2,10},{10... | collective-permute-start | bytes 1572872 | tf_op jit(solution)/shard_map/ppermute | solution.py:655
  374.1 11.0 %collective-permute-start.29 = (bf16[256,1024]{1,0:T(8,128)(2,1)S(1)}, bf16[256,1024]{1,0:T(8,128)(2,1)S(1)}, u32[]{:S(2)}, u32[]{:S(2)}) collective-permute-start(bf16[256,1024]{1,0:T(8,128)(2,1)S(1)} %collective-permute-done.27.refs_1_), channel_id=1, source_target_pairs={{0,8},{8,0},{16,24},{24,16},{1,9},{9,1},{17,25},{25,17},{2,10},{10... | collective-permute-start | bytes 1572872 | tf_op jit(solution)/shard_map/ppermute | solution.py:655
  374.1 22.8 %collective-permute-start.36 = (bf16[256,1024]{1,0:T(8,128)(2,1)S(1)}, bf16[256,1024]{1,0:T(8,128)(2,1)S(1)}, u32[]{:S(2)}, u32[]{:S(2)}) collective-permute-start(bf16[256,1024]{1,0:T(8,128)(2,1)S(1)} %add_convert_fusion.3.refs_0_), channel_id=1, source_target_pairs={{0,8},{8,0},{16,24},{24,16},{1,9},{9,1},{17,25},{25,17},{2,10},{10... | collective-permute-start | bytes 1572872 | tf_op jit(solution)/shard_map/ppermute | solution.py:655
  384.9 12.0 %collective-permute-start.37 = (bf16[256,1024]{1,0:T(8,128)(2,1)S(1)}, bf16[256,1024]{1,0:T(8,128)(2,1)S(1)}, u32[]{:S(2)}, u32[]{:S(2)}) collective-permute-start(bf16[256,1024]{1,0:T(8,128)(2,1)S(1)} %collective-permute-done.35.refs_1_), channel_id=1, source_target_pairs={{0,8},{8,0},{16,24},{24,16},{1,9},{9,1},{17,25},{25,17},{2,10},{10... | collective-permute-start | bytes 1572872 | tf_op jit(solution)/shard_map/ppermute | solution.py:655
  423.7 8.6 %collective-permute-start.39 = (bf16[256,1024]{1,0:T(8,128)(2,1)}, bf16[256,1024]{1,0:T(8,128)(2,1)}, u32[]{:S(2)}, u32[]{:S(2)}) collective-permute-start(bf16[256,1024]{1,0:T(8,128)(2,1)} %get-tuple-element.154), channel_id=1, source_target_pairs={{0,8},{8,0},{16,24},{24,16},{1,9},{9,1},{17,25},{25,17},{2,10},{10... | collective-permute-start | bytes 1572872 | tf_op jit(solution)/shard_map/ppermute | solution.py:655
  427.9 9.0 %collective-permute-start.42 = (bf16[256,1024]{1,0:T(8,128)(2,1)}, bf16[256,1024]{1,0:T(8,128)(2,1)}, u32[]{:S(2)}, u32[]{:S(2)}) collective-permute-start(bf16[256,1024]{1,0:T(8,128)(2,1)} %get-tuple-element.162), channel_id=1, source_target_pairs={{0,8},{8,0},{16,24},{24,16},{1,9},{9,1},{17,25},{25,17},{2,10},{10... | collective-permute-start | bytes 1572872 | tf_op jit(solution)/shard_map/ppermute | solution.py:655
  431.8 6.5 %collective-permute-start.38 = (bf16[256,1024]{1,0:T(8,128)(2,1)S(1)}, bf16[256,1024]{1,0:T(8,128)(2,1)S(1)}, u32[]{:S(2)}, u32[]{:S(2)}) collective-permute-start(bf16[256,1024]{1,0:T(8,128)(2,1)S(1)} %get-tuple-element.149), channel_id=1, source_target_pairs={{0,8},{8,0},{16,24},{24,16},{1,9},{9,1},{17,25},{25,17},{2,10},{10... | collective-permute-start | bytes 1572872 | tf_op jit(solution)/shard_map/ppermute | solution.py:655
  433.7 26.7 %collective-permute-start.41 = (bf16[256,1024]{1,0:T(8,128)(2,1)S(1)}, bf16[256,1024]{1,0:T(8,128)(2,1)S(1)}, u32[]{:S(2)}, u32[]{:S(2)}) collective-permute-start(bf16[256,1024]{1,0:T(8,128)(2,1)S(1)} %add_convert_fusion.1), channel_id=1, source_target_pairs={{0,16},{8,24},{1,17},{9,25},{2,18},{10,26},{3,19},{11,27},{4,20},{... | collective-permute-start | bytes 1572872 | tf_op jit(solution)/shard_map/ppermute | solution.py:906
  438.2 22.2 %collective-permute-start.43 = (bf16[256,1024]{1,0:T(8,128)(2,1)S(1)}, bf16[256,1024]{1,0:T(8,128)(2,1)S(1)}, u32[]{:S(2)}, u32[]{:S(2)}) collective-permute-start(bf16[256,1024]{1,0:T(8,128)(2,1)S(1)} %add_convert_fusion.refs_0_), channel_id=1, source_target_pairs={{0,16},{8,24},{16,0},{24,8},{1,17},{9,25},{17,1},{25,9},{2,18},{10... | collective-permute-start | bytes 1572872 | tf_op jit(solution)/shard_map/ppermute | solution.py:658
  438.5 25.8 %collective-permute-start.40 = (bf16[256,1024]{1,0:T(8,128)(2,1)S(1)}, bf16[256,1024]{1,0:T(8,128)(2,1)S(1)}, u32[]{:S(2)}, u32[]{:S(2)}) collective-permute-start(bf16[256,1024]{1,0:T(8,128)(2,1)S(1)} %add_convert_fusion.2), channel_id=1, source_target_pairs={{16,0},{24,8},{17,1},{25,9},{18,2},{26,10},{19,3},{27,11},{20,4},{... | collective-permute-start | bytes 1572872 | tf_op jit(solution)/shard_map/ppermute | solution.py:906
  440.3 29.3 %collective-permute-start.52 = (bf16[512,256]{1,0:T(8,128)(2,1)S(1)}, bf16[512,256]{1,0:T(8,128)(2,1)S(1)}, u32[]{:S(2)}, u32[]{:S(2)}) collective-permute-start(bf16[512,256]{1,0:T(8,128)(2,1)S(1)} %copy-done.48), channel_id=1, source_target_pairs={{0,16},{8,24},{16,0},{24,8},{1,17},{9,25},{17,1},{25,9},{2,18},{10... | collective-permute-start | bytes 786440 | tf_op jit(solution)/shard_map/ppermute | solution.py:658
  443.0 22.8 %collective-permute-start.44 = (bf16[256,1024]{1,0:T(8,128)(2,1)S(1)}, bf16[256,1024]{1,0:T(8,128)(2,1)S(1)}, u32[]{:S(2)}, u32[]{:S(2)}) collective-permute-start(bf16[256,1024]{1,0:T(8,128)(2,1)S(1)} %add_convert_fusion.refs_0_), channel_id=1, source_target_pairs={{0,8},{8,0},{16,24},{24,16},{1,9},{9,1},{17,25},{25,17},{2,10},{10... | collective-permute-start | bytes 1572872 | tf_op jit(solution)/shard_map/ppermute | solution.py:655
  474.1 6.5 %collective-permute-start.48 = (f32[4,1024]{1,0:T(4,128)S(1)}, f32[4,1024]{1,0:T(4,128)S(1)}, u32[]{:S(2)}, u32[]{:S(2)}) collective-permute-start(f32[4,1024]{1,0:T(4,128)S(1)} %fusion.20), channel_id=1, source_target_pairs={{0,1},{1,0},{2,3},{3,2},{4,5},{5,4},{6,7},{7,6},{8,9},{9,8},{10,11... | collective-permute-start | bytes 49160 | tf_op jit(solution)/shard_map/ppermute | solution.py:692
  (138 other events, 1087.2 us)
Sparse Core Ops, SparseCore 0:
  10.8 57.3 all-gather.5
  71.0 59.0 all-gather.3
  132.2 72.4 all-gather.7
  316.1 86.0 reduce-scatter.4
  417.3 87.0 reduce-scatter.2
